TPU v7x, 32 devices: a whole 2x2x4 slice. The times are simulated.
32 devices in a mesh: rows: 8 (over z, x), scales: 4 (over y, core).
Axes of the slice: x: 2, y: 2, z: 4, core: 2. Of those that a mesh axis runs over, the one named last changes fastest.
Arguments:
- image_now: float32 [256, 8192], P(('rows', 'scales')), may hold values from 0.1 to 4
- gradient: float32 [256, 8192], P(('rows', 'scales')), may hold values from -140 to 140
- hessian_weight: float32 [256, 8192], P(('rows', 'scales')), may hold values from 0.1 to 10
- psf_tiles: float32 [32, 256], P(('rows', 'scales')), may hold values from -0.5 to 1.7
- facet_of_row: int32 [256], P(('rows', 'scales')), may hold values from 0 to 31, never falling along the last dimension, each value on 1 to 32 neighbouring positions
- tile_slot: int32 [32], replicated, may hold values from 0 to 31, each once
- thresholds: float32 [4], replicated, may hold values from 0.2 to 2
Outputs:
- new_image: float32 [256, 8192], P(('rows', 'scales'))
Inputs may be any that keep to these rules, and one draw needn't show every extreme that they name: `facet_of_row`: facet numbers never fall along the rows; every facet covers 1 to 32 rows, and some facet exactly 32. `tile_slot`: each facet's tile stands in a different row of psf_tiles, and every row holds one.
All inputs are finite; a program needn't handle non-finite values.
Results may differ from a plain program's by a relative error of at most 0.0001.
Values sent between devices are 32-bit elements; how exact they have to be, the bound alone decides.
A program may use at most 64 MiB of HBM per device.

v0:
```python
import jax
import jax.numpy as jnp
from jax import lax
from jax.sharding import PartitionSpec as P

TILE = 16
SUBITERS = 2


SPLINE_EDGE = 0.0625
SPLINE_NEAR = 0.25
SPLINE_MID = 0.375


def padded_2(cells, sides, width):
    for axis, dim in sides:
        count = lax.axis_size(axis)
        ends = count - 1
        head = lax.slice_in_dim(cells, 0, width, axis=dim)
        tail = lax.slice_in_dim(cells, cells.shape[dim] - width, cells.shape[dim], axis=dim)
        cells = jnp.concatenate(
            [
                lax.ppermute(tail, axis, [(i, (i + 1) % count) for i in range(ends)]),
                cells,
                lax.ppermute(head, axis, [((i + 1) % count, i) for i in range(ends)]),
            ],
            axis=dim,
        )
    return cells


def along_columns(source, spacing):
    length = source.shape[1]
    padded = jnp.pad(source, ((0, 0), (2 * spacing, 2 * spacing)))
    outer_pair = padded[:, 0:length] + padded[:, 4 * spacing : 4 * spacing + length]
    inner_pair = (
        padded[:, spacing : spacing + length] + padded[:, 3 * spacing : 3 * spacing + length]
    )
    return SPLINE_EDGE * outer_pair + SPLINE_NEAR * inner_pair + SPLINE_MID * source


def rows_traced(source, spacing, reach):
    length = source.shape[0]
    padded = jnp.pad(source, ((reach, reach), (0, 0)))

    def shifted_rows(offset):
        return lax.dynamic_slice_in_dim(padded, reach + offset, length, 0)

    outer_pair = shifted_rows(-2 * spacing) + shifted_rows(2 * spacing)
    inner_pair = shifted_rows(-spacing) + shifted_rows(spacing)
    return SPLINE_EDGE * outer_pair + SPLINE_NEAR * inner_pair + SPLINE_MID * source


def widen_band(source):
    half_tile = TILE // 2
    extended = padded_2(source, ((("rows", "scales"), 0),), half_tile)
    return jnp.pad(extended, ((0, 0), (half_tile, half_tile)))


def forward_blur(source, weights):
    band_rows, columns = source.shape
    padded = widen_band(source)

    def forward_add_tap_row(tap_row, summed):
        shifted = lax.dynamic_slice_in_dim(padded, tap_row, band_rows, 0)
        tap_weights = lax.dynamic_index_in_dim(weights, tap_row, 1, keepdims=False)
        for column in range(TILE):
            summed = (
                summed + tap_weights[:, column : column + 1] * shifted[:, column : column + columns]
            )
        return summed

    return lax.fori_loop(0, TILE, forward_add_tap_row, jnp.zeros((band_rows, columns), jnp.float32))


def adjoint_blur(source, wide_weights):
    band_rows, columns = source.shape
    half_tile = TILE // 2
    padded = widen_band(source)

    def adjoint_add_tap_row(tap_row, summed):
        offset = 2 * half_tile - tap_row
        shifted = lax.dynamic_slice_in_dim(padded, offset, band_rows, 0)
        weight_rows = lax.dynamic_slice_in_dim(wide_weights, offset, band_rows, 0)
        tap_weights = lax.dynamic_index_in_dim(weight_rows, tap_row, 1, keepdims=False)
        for column in range(TILE):
            offset_col = 2 * half_tile - column
            summed = (
                summed
                + tap_weights[:, column : column + 1]
                * shifted[:, offset_col : offset_col + columns]
            )
        return summed

    return lax.fori_loop(0, TILE, adjoint_add_tap_row, jnp.zeros((band_rows, columns), jnp.float32))


def body(image_now, gradient, hessian_weight, psf_tiles, facet_of_row, tile_slot, thresholds):
    band_rows, columns = image_now.shape
    half_tile = TILE // 2
    scale_count = lax.axis_size("scales")
    scale_index = lax.axis_index("scales")
    facet_ids = jnp.arange(tile_slot.shape[0], dtype=jnp.int32)
    slot_rows = jnp.sum(
        jnp.where(facet_of_row[:, None] == facet_ids[None, :], tile_slot[None, :], 0), axis=1
    )
    tiles_in = lax.all_gather(psf_tiles, ("rows", "scales"), axis=0, tiled=True)
    length = tiles_in.shape[0]
    onehot = (slot_rows[:, None] == jnp.arange(length, dtype=jnp.int32)[None, :]).astype(
        jnp.float32
    )
    flat_rows = jnp.dot(
        onehot, tiles_in, precision=lax.Precision.HIGHEST, preferred_element_type=jnp.float32
    )
    wide_rows = padded_2(flat_rows, ((("rows", "scales"), 0),), half_tile)
    weights = flat_rows.reshape(band_rows, TILE, TILE)
    wide_weights = wide_rows.reshape(band_rows + 2 * half_tile, TILE, TILE)
    level_gain = jnp.sum(jnp.where(jnp.arange(scale_count) == scale_index, thresholds, 0.0))
    reach = 2**scale_count

    def column_level(depth, plane):
        return rows_traced(plane, jnp.left_shift(jnp.int32(1), depth), reach)

    current = image_now
    for sweep in range(SUBITERS):
        change = current - image_now
        pushed = hessian_weight * forward_blur(change, weights)
        descent = gradient + adjoint_blur(pushed, wide_weights)
        blurred = forward_blur(descent, weights)
        totals = lax.psum(
            (jnp.sum(descent * descent), jnp.sum(hessian_weight * blurred * blurred)),
            ("rows", "scales"),
        )
        step_size = totals[0] / totals[1]
        trial = current - step_size * descent
        stripe = lax.all_gather(trial, "scales", axis=0, tiled=True)
        smooth = stripe
        lower = jnp.zeros_like(stripe)
        upper = jnp.zeros_like(stripe)
        for depth in range(scale_count):
            smoother = along_columns(smooth, 2**depth)
            lower = jnp.where(scale_index == depth, smooth, lower)
            upper = jnp.where(scale_index == depth, smoother, upper)
            smooth = smoother
        limit = step_size * level_gain
        lower_cols, upper_cols = (
            lax.all_to_all(lower, "rows", split_axis=1, concat_axis=0, tiled=True),
            lax.all_to_all(upper, "rows", split_axis=1, concat_axis=0, tiled=True),
        )
        lower_cols = lax.fori_loop(0, scale_index, column_level, lower_cols)
        upper_cols = lax.fori_loop(0, scale_index + 1, column_level, upper_cols)
        detail = lower_cols - upper_cols
        kept = (
            detail
            - jnp.clip(detail, -limit, limit)
            + jnp.where(scale_index == scale_count - 1, upper_cols, 0.0)
        )
        contribution = lax.all_to_all(kept, "rows", split_axis=0, concat_axis=1, tiled=True)
        current = lax.psum_scatter(contribution, "scales", scatter_dimension=0, tiled=True)
    return current


def solution(mesh):
    in_specs = (
        P(("rows", "scales"), None),
        P(("rows", "scales"), None),
        P(("rows", "scales"), None),
        P(("rows", "scales"), None),
        P(("rows", "scales")),
        P(),
        P(),
    )
    out_specs = P(("rows", "scales"), None)
    return jax.shard_map(body, mesh=mesh, in_specs=in_specs, out_specs=out_specs, check_vma=False)
```

profile of v0, /device:TPU:1, one launch (start us, length us, event | category | flops | bytes accessed | tf_op | source)
XLA Modules:
  0.0 671.9 jit_solution(16924233468898300590)
XLA Ops:
  7.6 4.5 collective-permute-start.2
  12.1 1.9 collective-permute-start.3
  14.9 42.6 %all-gather = f32[32,1,256]{2,1,0:T(1,128)S(1)} all-gather(f32[1,1,256]{2,1,0:T(1,128)} %bitcast.79), channel_id=1, replica_groups=mesh['rows'=8,'scales'=4] {'rows','scales'}, dimensions={0}, use_global_device_ids=true | all-gather | bytes 33792 | tf_op jit(solution)/shard_map/all_gather | solution.py:107
  58.1 27.8 %while.146 = (s32[]{:T(128)}, f32[8,8192]{1,0:T(8,128)S(1)}, f32[8,16,16]{2,0,1:T(8,128)S(1)}, f32[24,8208]{1,0:T(8,128)S(1)}, s32[]{:T(128)}, /*index=5*/s32[]{...) while((s32[]{:T(128)}, f32[8,8192]{1,0:T(8,128)S(1)}, ...), condition=%wide.region_2.3_spmd.clone, body=%wide.region_1.2_spmd.clone.sunk | while | flops 2162706 | bytes 4721599 | solution.py:73
  85.9 1.9 collective-permute-start.4
  87.9 2.4 collective-permute-start.5
  90.3 3.1 collective-permute-start
  93.4 1.9 collective-permute-start.1
  95.4 3.0 collective-permute-done.1
  98.9 29.6 %while.147 = (s32[]{:T(128)}, f32[8,8192]{1,0:T(8,128)S(1)}, f32[24,16,16]{2,0,1:T(8,128)S(1)}, f32[24,8208]{1,0:T(8,128)S(1)}, s32[]{:T(128)}, /*index=5*/s32[]...) while((s32[]{:T(128)}, f32[8,8192]{1,0:T(8,128)S(1)}, ...), condition=%wide.region_4.5_spmd.clone, body=%wide.region_3.4_spmd.clone.sunk | while | flops 2162713 | bytes 4721729 | solution.py:95
  101.2 1.4 fusion.159
  103.1 1.4 fusion.159
  104.9 1.4 fusion.159
  106.8 1.4 fusion.159
  108.7 1.4 fusion.159
  110.5 1.4 fusion.159
  112.4 1.4 fusion.159
  114.2 1.4 fusion.159
  129.2 1.9 collective-permute-start.6
  131.1 2.4 collective-permute-start.7
  134.4 4.4 collective-permute-done.7
  139.1 27.8 %while.148 = (s32[]{:T(128)}, f32[8,8192]{1,0:T(8,128)S(1)}, f32[8,16,16]{2,0,1:T(8,128)S(1)}, f32[24,8208]{1,0:T(8,128)S(1)}, s32[]{:T(128)}, /*index=5*/s32[]{...) while((s32[]{:T(128)}, f32[8,8192]{1,0:T(8,128)S(1)}, ...), condition=%wide.region_8.9_spmd.clone, body=%wide.region_7.8_spmd.clone.sunk | while | flops 2162706 | bytes 4721599 | solution.py:73
  167.7 37.4 %all-reduce.19 = (f32[]{:T(128)}, f32[]{:T(128)}) all-reduce(f32[]{:T(128)} %get-tuple-element.1221, f32[]{:T(128)} %fusion.137), channel_id=1, replica_groups=mesh['rows'=8,'scales'=4] {'rows','scales'}, use_global_device_ids=true, to_apply=%region_6.7 | all-reduce | flops 2 | bytes 16 | tf_op jit(solution)/shard_map/psum | solution.py:130
  207.3 18.3 %all-gather.4.cloned.1.call-done = f32[32,8192]{1,0:T(8,128)} async-done(((f32[8,8192]{1,0:T(8,128)}), f32[32,8192]{1,0:T(8,128)}) %all-gather.4.cloned.1.call-update) | async-done | bytes 1048592 | tf_op jit(solution)/shard_map/all_gather | solution.py:136
  225.6 4.2 multiply_add_fusion.5
  231.0 2.2 select_select_fusion.3
  233.2 2.3 select_select_fusion.2
  236.6 5.2 all-to-all-start.1
  242.9 24.3 %all-to-all-done.1 = f32[32,8,1024]{2,0,1:T(8,128)S(1)} async-done(((f32[32,8,1024]{2,0,1:T(8,128)}), f32[32,8,1024]{2,0,1:T(8,128)S(1)}, u32[]{:S(2)}, u32[]{:S(2)}) %all-to-all-start.1) | async-done | bytes 1048608 | tf_op jit(solution)/shard_map/all_to_all | solution.py:148
  267.2 4.4 all-to-all-start
  272.8 1.7 while.143
  274.5 22.2 %all-to-all-done = f32[32,8,1024]{2,0,1:T(8,128)S(1)} async-done(((f32[32,8,1024]{2,0,1:T(8,128)}), f32[32,8,1024]{2,0,1:T(8,128)S(1)}, u32[]{:S(2)}, u32[]{:S(2)}) %all-to-all-start) | async-done | bytes 1048608 | tf_op jit(solution)/shard_map/all_to_all | solution.py:147
  297.8 29.8 %all_to_all.114 = f32[8,32,1024]{2,1,0:T(8,128)S(1)} all-to-all(f32[8,32,1024]{2,1,0:T(8,128)S(1)} %bitcast.72), channel_id=1, replica_groups=mesh['rows'=8,'scales'=4] {'rows'}, dimensions={0} | all-to-all | bytes 2097152 | tf_op jit(solution)/shard_map/all_to_all | solution.py:158
  328.8 25.0 %reduce-scatter.3.cloned.1.call-done = f32[8,8192]{1,0:T(8,128)} async-done(((f32[32,8192]{1,0:T(8,128)}), f32[8,8192]{1,0:T(8,128)}) %reduce-scatter.3.cloned.1.call-update) | async-done | bytes 262160 | tf_op jit(solution)/shard_map/reduce_scatter | solution.py:159
  354.7 2.7 collective-permute-start.8
  357.5 1.9 collective-permute-start.9
  360.7 4.4 collective-permute-done.9
  365.4 27.8 %while.149 = (s32[]{:T(128)}, f32[8,8192]{1,0:T(8,128)S(1)}, f32[8,16,16]{2,0,1:T(8,128)S(1)}, f32[24,8208]{1,0:T(8,128)S(1)}, s32[]{:T(128)}, /*index=5*/s32[]{...) while((s32[]{:T(128)}, f32[8,8192]{1,0:T(8,128)S(1)}, ...), condition=%wide.region_18.19_spmd.clone, body=%wide.region_17.18_spmd.clone.sunk | while | flops 2162706 | bytes 4721599 | solution.py:73
  393.3 1.9 collective-permute-start.10
  395.2 2.6 collective-permute-start.11
  398.5 6.3 collective-permute-done.11
  405.0 29.6 %while.150 = (s32[]{:T(128)}, f32[8,8192]{1,0:T(8,128)S(1)}, f32[24,16,16]{2,0,1:T(8,128)S(1)}, f32[24,8208]{1,0:T(8,128)S(1)}, s32[]{:T(128)}, /*index=5*/s32[]...) while((s32[]{:T(128)}, f32[8,8192]{1,0:T(8,128)S(1)}, ...), condition=%wide.region_20.21_spmd.clone, body=%wide.region_19.20_spmd.clone.sunk | while | flops 2162713 | bytes 4721729 | solution.py:95
  407.4 1.4 fusion.162
  409.2 1.4 fusion.162
  411.1 1.4 fusion.162
  412.9 1.4 fusion.162
  414.8 1.4 fusion.162
  420.3 1.4 fusion.162
  435.3 1.9 collective-permute-start.12
  437.2 2.4 collective-permute-start.13
  440.5 5.3 collective-permute-done.13
  446.1 27.8 %while.151 = (s32[]{:T(128)}, f32[8,8192]{1,0:T(8,128)S(1)}, f32[8,16,16]{2,0,1:T(8,128)S(1)}, f32[24,8208]{1,0:T(8,128)S(1)}, s32[]{:T(128)}, /*index=5*/s32[]{...) while((s32[]{:T(128)}, f32[8,8192]{1,0:T(8,128)S(1)}, ...), condition=%wide.region_24.25_spmd.clone, body=%wide.region_23.24_spmd.clone.sunk | while | flops 2162706 | bytes 4721599 | solution.py:73
  474.6 41.5 %all-reduce.18 = (f32[]{:T(128)}, f32[]{:T(128)}) all-reduce(f32[]{:T(128)} %get-tuple-element.1217, f32[]{:T(128)} %fusion.138), channel_id=1, replica_groups=mesh['rows'=8,'scales'=4] {'rows','scales'}, use_global_device_ids=true, to_apply=%region_22.23 | all-reduce | flops 2 | bytes 16 | tf_op jit(solution)/shard_map/psum | solution.py:130
  518.2 19.2 %all-gather.6.cloned.1.call-done = f32[32,8192]{1,0:T(8,128)} async-done(((f32[8,8192]{1,0:T(8,128)}), f32[32,8192]{1,0:T(8,128)}) %all-gather.6.cloned.1.call-update) | async-done | bytes 1048592 | tf_op jit(solution)/shard_map/all_gather | solution.py:136
  537.4 4.2 multiply_add_fusion.2
  542.8 2.2 select_select_fusion.1
  545.0 2.2 select_select_fusion
  548.3 5.2 all-to-all-start.4
  554.6 24.3 %all-to-all-done.4 = f32[32,8,1024]{2,0,1:T(8,128)S(1)} async-done(((f32[32,8,1024]{2,0,1:T(8,128)}), f32[32,8,1024]{2,0,1:T(8,128)S(1)}, u32[]{:S(2)}, u32[]{:S(2)}) %all-to-all-start.4) | async-done | bytes 1048608 | tf_op jit(solution)/shard_map/all_to_all | solution.py:148
  578.9 4.2 all-to-all-start.3
  583.8 1.7 while.145
  585.5 22.8 %all-to-all-done.3 = f32[32,8,1024]{2,0,1:T(8,128)S(1)} async-done(((f32[32,8,1024]{2,0,1:T(8,128)}), f32[32,8,1024]{2,0,1:T(8,128)S(1)}, u32[]{:S(2)}, u32[]{:S(2)}) %all-to-all-start.3) | async-done | bytes 1048608 | tf_op jit(solution)/shard_map/all_to_all | solution.py:147
  609.4 29.8 %all_to_all.115 = f32[8,32,1024]{2,1,0:T(8,128)S(1)} all-to-all(f32[8,32,1024]{2,1,0:T(8,128)S(1)} %bitcast.71), channel_id=1, replica_groups=mesh['rows'=8,'scales'=4] {'rows'}, dimensions={0} | all-to-all | bytes 2097152 | tf_op jit(solution)/shard_map/all_to_all | solution.py:158
  640.3 25.1 %reduce-scatter.5.cloned.1.call-done = f32[8,8192]{1,0:T(8,128)} async-done(((f32[32,8192]{1,0:T(8,128)}), f32[8,8192]{1,0:T(8,128)}) %reduce-scatter.5.cloned.1.call-update) | async-done | bytes 262160 | tf_op jit(solution)/shard_map/reduce_scatter | solution.py:159
  (359 shorter events, 177.6 us)
Async XLA Ops:
  6.5 219.0 %all-gather.4.cloned.1.call-start = ((), (), s32[]{:S(2)}) async-start(), calls=%async_computation.8 | async-start | bytes 1310720 | tf_op jit(solution)/shard_map/all_gather | solution.py:136
  7.6 50.2 %collective-permute-start.2 = (f32[8,8192]{1,0:T(8,128)S(1)}, f32[8,8192]{1,0:T(8,128)S(1)}, u32[]{:S(2)}, u32[]{:S(2)}) collective-permute-start(f32[8,8192]{1,0:T(8,128)S(1)} %sub.46), channel_id=1, source_target_pairs={{0,1},{1,2},{2,3},{3,4},{4,5},{5,6},{6,7},{7,8},{8,9},{9,10},{10,1... | collective-permute-start | bytes 786440 | tf_op jit(solution)/shard_map/ppermute | solution.py:23
  12.1 45.7 %collective-permute-start.3 = (f32[8,8192]{1,0:T(8,128)S(1)}, f32[8,8192]{1,0:T(8,128)S(1)}, u32[]{:S(2)}, u32[]{:S(2)}) collective-permute-start(f32[8,8192]{1,0:T(8,128)S(1)} %sub.46), channel_id=1, source_target_pairs={{1,0},{2,1},{3,2},{4,3},{5,4},{6,5},{7,6},{8,7},{9,8},{10,9},{11,1... | collective-permute-start | bytes 786440 | tf_op jit(solution)/shard_map/ppermute | solution.py:25
  58.1 27.8 %copy-start = (f32[8,8192]{1,0:T(8,128)S(1)}, f32[8,8192]{1,0:T(8,128)}, u32[]{:S(2)}) copy-start(f32[8,8192]{1,0:T(8,128)} %param.29) | copy-start | bytes 786436
  85.9 12.7 %collective-permute-start.4 = (f32[8,8192]{1,0:T(8,128)S(1)}, f32[8,8192]{1,0:T(8,128)S(1)}, u32[]{:S(2)}, u32[]{:S(2)}) collective-permute-start(f32[8,8192]{1,0:T(8,128)S(1)} %mul.2942), channel_id=1, source_target_pairs={{0,1},{1,2},{2,3},{3,4},{4,5},{5,6},{6,7},{7,8},{8,9},{9,10},{10,1... | collective-permute-start | bytes 786440 | tf_op jit(solution)/shard_map/ppermute | solution.py:23
  87.9 10.8 %collective-permute-start.5 = (f32[8,8192]{1,0:T(8,128)S(1)}, f32[8,8192]{1,0:T(8,128)S(1)}, u32[]{:S(2)}, u32[]{:S(2)}) collective-permute-start(f32[8,8192]{1,0:T(8,128)S(1)} %mul.2942), channel_id=1, source_target_pairs={{1,0},{2,1},{3,2},{4,3},{5,4},{6,5},{7,6},{8,7},{9,8},{10,9},{11,1... | collective-permute-start | bytes 786440 | tf_op jit(solution)/shard_map/ppermute | solution.py:25
  90.3 5.1 collective-permute-start
  93.4 5.0 collective-permute-start.1
  98.9 29.6 %copy-start.5 = (f32[8,8192]{1,0:T(8,128)S(1)}, f32[8,8192]{1,0:T(8,128)}, u32[]{:S(2)}) copy-start(f32[8,8192]{1,0:T(8,128)} %param.28) | copy-start | bytes 786436
  129.2 5.2 collective-permute-start.6
  131.1 7.7 %collective-permute-start.7 = (f32[8,8192]{1,0:T(8,128)S(1)}, f32[8,8192]{1,0:T(8,128)S(1)}, u32[]{:S(2)}, u32[]{:S(2)}) collective-permute-start(f32[8,8192]{1,0:T(8,128)S(1)} %get-tuple-element.1222), channel_id=1, source_target_pairs={{1,0},{2,1},{3,2},{4,3},{5,4},{6,5},{7,6},{8,7},{9,8},{10,9},{11,1... | collective-permute-start | bytes 786440 | tf_op jit(solution)/shard_map/ppermute | solution.py:25
  139.1 67.4 %copy-start.1 = (f32[8,8192]{1,0:T(8,128)S(1)}, f32[8,8192]{1,0:T(8,128)}, u32[]{:S(2)}) copy-start(f32[8,8192]{1,0:T(8,128)} %param.27) | copy-start | bytes 786436
  229.7 1.2 copy-start.2
  236.6 30.6 %all-to-all-start.1 = ((f32[32,8,1024]{2,0,1:T(8,128)}), f32[32,8,1024]{2,0,1:T(8,128)S(1)}, u32[]{:S(2)}, u32[]{:S(2)}) async-start(f32[32,8,1024]{2,0,1:T(8,128)} %bitcast.50), calls=%async_computation.1 | async-start | bytes 2097152 | tf_op jit(solution)/shard_map/all_to_all | solution.py:148
  267.2 4.4 copy-start.6
  267.2 29.5 %all-to-all-start = ((f32[32,8,1024]{2,0,1:T(8,128)}), f32[32,8,1024]{2,0,1:T(8,128)S(1)}, u32[]{:S(2)}, u32[]{:S(2)}) async-start(f32[32,8,1024]{2,0,1:T(8,128)} %bitcast.68), calls=%async_computation | async-start | bytes 2097152 | tf_op jit(solution)/shard_map/all_to_all | solution.py:147
  271.5 82.2 %reduce-scatter.3.cloned.1.call-start = ((), (), s32[]{:S(2)}) async-start(), calls=%async_computation.9 | async-start | bytes 1310720 | tf_op jit(solution)/shard_map/reduce_scatter | solution.py:159
  328.7 208.7 %all-gather.6.cloned.1.call-start = ((), (), s32[]{:S(2)}) async-start(), calls=%async_computation.10 | async-start | bytes 1310720 | tf_op jit(solution)/shard_map/all_gather | solution.py:136
  354.7 6.0 collective-permute-start.8
  357.5 7.7 %collective-permute-start.9 = (f32[8,8192]{1,0:T(8,128)S(1)}, f32[8,8192]{1,0:T(8,128)S(1)}, u32[]{:S(2)}, u32[]{:S(2)}) collective-permute-start(f32[8,8192]{1,0:T(8,128)S(1)} %sub.50), channel_id=1, source_target_pairs={{1,0},{2,1},{3,2},{4,3},{5,4},{6,5},{7,6},{8,7},{9,8},{10,9},{11,1... | collective-permute-start | bytes 786440 | tf_op jit(solution)/shard_map/ppermute | solution.py:25
  393.3 5.2 collective-permute-start.10
  395.2 9.6 %collective-permute-start.11 = (f32[8,8192]{1,0:T(8,128)S(1)}, f32[8,8192]{1,0:T(8,128)S(1)}, u32[]{:S(2)}, u32[]{:S(2)}) collective-permute-start(f32[8,8192]{1,0:T(8,128)S(1)} %mul.2961), channel_id=1, source_target_pairs={{1,0},{2,1},{3,2},{4,3},{5,4},{6,5},{7,6},{8,7},{9,8},{10,9},{11,1... | collective-permute-start | bytes 786440 | tf_op jit(solution)/shard_map/ppermute | solution.py:25
  435.3 5.2 collective-permute-start.12
  437.2 8.6 %collective-permute-start.13 = (f32[8,8192]{1,0:T(8,128)S(1)}, f32[8,8192]{1,0:T(8,128)S(1)}, u32[]{:S(2)}, u32[]{:S(2)}) collective-permute-start(f32[8,8192]{1,0:T(8,128)S(1)} %get-tuple-element.1218), channel_id=1, source_target_pairs={{1,0},{2,1},{3,2},{4,3},{5,4},{6,5},{7,6},{8,7},{9,8},{10,9},{11,1... | collective-permute-start | bytes 786440 | tf_op jit(solution)/shard_map/ppermute | solution.py:25
  446.1 71.4 %copy-start.4 = (f32[8,8192]{1,0:T(8,128)S(1)}, f32[8,8192]{1,0:T(8,128)}, u32[]{:S(2)}) copy-start(f32[8,8192]{1,0:T(8,128)} %reduce-scatter.3.cloned.1.call-done) | copy-start | bytes 786436
  541.5 1.2 copy-start.3
  548.3 30.6 %all-to-all-start.4 = ((f32[32,8,1024]{2,0,1:T(8,128)}), f32[32,8,1024]{2,0,1:T(8,128)S(1)}, u32[]{:S(2)}, u32[]{:S(2)}) async-start(f32[32,8,1024]{2,0,1:T(8,128)} %bitcast.48), calls=%async_computation.5 | async-start | bytes 2097152 | tf_op jit(solution)/shard_map/all_to_all | solution.py:148
  578.9 29.4 %all-to-all-start.3 = ((f32[32,8,1024]{2,0,1:T(8,128)}), f32[32,8,1024]{2,0,1:T(8,128)S(1)}, u32[]{:S(2)}, u32[]{:S(2)}) async-start(f32[32,8,1024]{2,0,1:T(8,128)} %bitcast.49), calls=%async_computation.4 | async-start | bytes 2097152 | tf_op jit(solution)/shard_map/all_to_all | solution.py:147
  583.1 82.2 %reduce-scatter.5.cloned.1.call-start = ((), (), s32[]{:S(2)}) async-start(), calls=%async_computation.11 | async-start | bytes 1310720 | tf_op jit(solution)/shard_map/reduce_scatter | solution.py:159
Sparse Core Ops, SparseCore 0:
  207.4 18.1 all-gather.3
  328.8 24.8 reduce-scatter.2
  518.3 18.9 all-gather.5
  640.4 24.8 reduce-scatter.4
where the time goes:
time: 674 us; the launch traced here: 672 us
  waiting for transfers between devices  208 us (31%)
  blocking collectives  181 us (27%)
  other arithmetic  158 us (23%)
  starting transfers between devices  52.9 us (8%)
  local copies, waits for them, and re-layouts  49.9 us (7%)
  between operations  17.6 us (3%)
    add x64, other arithmetic, forward_add_tap_row(): summed + tap_weights[:, column:column + 1] * shifted[:, column:column + c...  81 us
    psum x2, blocking collectives, body(): lax.psum((jnp.sum(descent * descent), jnp.sum(hessian_weight * blurred *...  78.9 us
    all_to_all x2, blocking collectives, body(): lax.all_to_all(kept, 'rows', split_axis=0, concat_axis=1, tiled=True)  59.6 us
    reduce_scatter x2, waiting for transfers between devices, body(): lax.psum_scatter(contribution, 'scales', scatter_dimension=0, tiled=True)  50.1 us
    all_to_all x2, waiting for transfers between devices, body(): lax.all_to_all(upper, 'rows', split_axis=1, concat_axis=0, tiled=True)  48.6 us
    all_to_all x2, waiting for transfers between devices, body(): lax.all_to_all(lower, 'rows', split_axis=1, concat_axis=0, tiled=True)  45 us
    add x32, other arithmetic, adjoint_add_tap_row(): summed + tap_weights[:, column:column + 1] * shifted[:, offset_col:offset...  43.6 us
    all_gather x1, blocking collectives, body(): tiles_in = lax.all_gather(psf_tiles, ('rows', 'scales'), axis=0, tiled=True)  42.6 us
  transfers between devices with their start and end apart: 22, of which 17 were waited for; matrix products, arithmetic and copies ran while one was open for 1% of the time, Pallas kernels for 0%

commit v1 on v0

v1 whole, which is shorter than its diff:
```python
import functools

import jax
import jax.numpy as jnp
import numpy as np
from jax import lax
from jax.experimental import pallas as pl
from jax.experimental.pallas import tpu as pltpu
from jax.sharding import PartitionSpec as P

TILE = 16
HALF = TILE // 2
SUBITERS = 2
LANES = 128
BLOCK = 32
GROUPS = LANES // BLOCK
WIDTH = 8 * BLOCK
AXES = ("rows", "scales")
VMEM = pl.BlockSpec(memory_space=pltpu.VMEM)


def spline_matrices(levels):
    w = np.arange(WIDTH)
    same = (w[:, None] // BLOCK) == (w[None, :] // BLOCK)
    offset = (w[:, None] % BLOCK) - (w[None, :] % BLOCK)
    planes = []
    for level in range(levels):
        d = 2**level
        for s in (-1, 0, 1):
            o = np.abs(offset + BLOCK * s)
            coef = np.where(o == 0, 0.375, np.where(o == d, 0.25, np.where(o == 2 * d, 0.0625, 0.0)))
            planes.append(np.where(same, coef, 0.0))
    return jnp.asarray(np.stack(planes), jnp.bfloat16)


def halves(x):
    high = x.astype(jnp.bfloat16)
    low = (x - high.astype(jnp.float32)).astype(jnp.bfloat16)
    return high, low


def dot(a, b):
    return jnp.dot(a, b, preferred_element_type=jnp.float32)


def block_shift(x, s):
    if s == 0:
        return x
    count = x.shape[0] // GROUPS
    parts = [x[p * count : (p + 1) * count] for p in range(GROUPS)]
    row = lax.broadcasted_iota(jnp.int32, parts[0].shape, 0)
    if s == 1:
        last = jnp.where(row == count - 1, 0.0, pltpu.roll(parts[0], count - 1, 0))
        return jnp.concatenate(parts[1:] + [last], axis=0)
    first = jnp.where(row == 0, 0.0, pltpu.roll(parts[-1], 1, 0))
    return jnp.concatenate([first] + parts[:-1], axis=0)


def blur(stripes, high_ref, low_ref):
    total = None
    for t, x in enumerate(stripes):
        for s in (-1, 0, 1):
            high, low = halves(block_shift(x, s))
            n = t * 3 + s + 1
            w = high_ref[n]
            part = dot(high, w) + dot(low, w) + dot(high, low_ref[n])
            total = part if total is None else total + part
    return total


def to_blocks(src_ref, dst_ref, tiles):
    count = src_ref.shape[1] // LANES
    for q in range(count):
        tiles[pl.ds(8 * q, 8), :] = src_ref[:, q * LANES : (q + 1) * LANES]
    group = lax.broadcasted_iota(jnp.int32, (count, LANES), 1) // BLOCK
    for half in range(2):
        outs = [None] * GROUPS
        for k in range(4):
            a = tiles[pl.ds(half * 4 + k, count, stride=8), :]
            for p in range(GROUPS):
                shift = BLOCK * ((k - p) % 4)
                moved = pltpu.roll(a, shift, 1) if shift else a
                outs[p] = moved if k == 0 else jnp.where(group == k, moved, outs[p])
        for p in range(GROUPS):
            dst_ref[p * count : (p + 1) * count, half * LANES : (half + 1) * LANES] = outs[p]


def from_blocks(src_ref, dst_ref, tiles):
    count = dst_ref.shape[1] // LANES
    group = lax.broadcasted_iota(jnp.int32, (count, LANES), 1) // BLOCK
    for half in range(2):
        for k in range(4):
            out = None
            for p in range(GROUPS):
                x = src_ref[p * count : (p + 1) * count, half * LANES : (half + 1) * LANES]
                shift = BLOCK * ((p - k) % 4)
                moved = pltpu.roll(x, shift, 1) if shift else x
                out = moved if p == 0 else jnp.where(group == p, moved, out)
            tiles[pl.ds(half * 4 + k, count, stride=8), :] = out
    for q in range(count):
        dst_ref[:, q * LANES : (q + 1) * LANES] = tiles[pl.ds(8 * q, 8), :]


def build_weights(base_ref, lead, high_ref, low_ref, wide):
    lane = lax.broadcasted_iota(jnp.int32, (8, WIDTH), 1) % BLOCK
    for t in range(3):
        base = base_ref[8 * t : 8 * t + 8, :]
        for w in range(BLOCK):
            for s in (-1, 0, 1):
                moved = pltpu.roll(base, (w - lead + BLOCK * s) % WIDTH, 1)
                x = lane - (w - lead + BLOCK * s)
                kept = jnp.where((x >= 0) & (x < TILE), moved, 0.0)
                for half in range(2):
                    wide[s + 1, half, pl.ds(w, 8, stride=BLOCK), :] = kept[
                        :, half * LANES : (half + 1) * LANES
                    ]
        for s in range(3):
            for half in range(2):
                high, low = halves(wide[s, half])
                high_ref[t * 3 + s, :, half * LANES : (half + 1) * LANES] = high
                low_ref[t * 3 + s, :, half * LANES : (half + 1) * LANES] = low


def moved_rows(vregs, rolls, i, d):
    if d % 4 == 0:
        return vregs[i + d // 4]
    shift = (-BLOCK * d) % LANES

    def rolled(n):
        if (n, shift) not in rolls:
            rolls[(n, shift)] = pltpu.roll(vregs[n], shift, 1)
        return rolls[(n, shift)]

    lane = lax.broadcasted_iota(jnp.int32, vregs[i].shape, 1)
    if d > 0:
        return jnp.where(lane < LANES - BLOCK * d, rolled(i), rolled(i + 1))
    return jnp.where(lane >= -BLOCK * d, rolled(i), rolled(i - 1))


def column_cascade(stripe_refs, alive, levels_ref, step_rows):
    reach = len(stripe_refs) // 2
    levels = levels_ref.shape[0]

    def chunk(n, carry):
        rows = pl.ds(pl.multiple_of(n * step_rows, step_rows), step_rows)
        vregs = {}
        for t, ref in enumerate(stripe_refs):
            for half in range(2):
                vregs[2 * t + half] = ref[rows, half * LANES : (half + 1) * LANES]
        own = 2 * reach
        for level in range(levels):
            d = 2**level
            left = 2 ** (levels + 1) - 2 ** (level + 2)
            margin = -(-left // 4)
            rolls, out = {}, {}
            keys = vregs
            for i in range(own - margin, own + 2 + margin):
                outer = moved_rows(keys, rolls, i, -2 * d) + moved_rows(keys, rolls, i, 2 * d)
                inner = moved_rows(keys, rolls, i, -d) + moved_rows(keys, rolls, i, d)
                value = 0.0625 * outer + 0.25 * inner + 0.375 * keys[i]
                t = i // 2
                out[i] = value if t == reach else value * alive[t]
            vregs = out
            for half in range(2):
                levels_ref[level, rows, half * LANES : (half + 1) * LANES] = out[own + half]
        return carry

    lax.fori_loop(0, stripe_refs[0].shape[0] // step_rows, chunk, 0)


def row_cascade(levels_ref, spline_ref):
    levels = levels_ref.shape[0]
    for level in range(levels):

        def one(k, carry):
            x = levels_ref[k]
            total = None
            for s in (-1, 0, 1):
                high, low = halves(block_shift(x, s))
                w = spline_ref[level * 3 + s + 1]
                part = dot(high, w) + dot(low, w)
                total = part if total is None else total + part
            levels_ref[k] = total
            return carry

        lax.fori_loop(level, levels, one, 0)


def keep(own, levels_ref, limits):
    levels = levels_ref.shape[0]
    smooth = own
    total = None
    for k in range(levels):
        smoother = levels_ref[k]
        detail = smooth - smoother
        part = detail - jnp.clip(detail, -limits[k], limits[k])
        total = part if total is None else total + part
        smooth = smoother
    return total + smooth


def prepare_kernel(image, gradient, weight, base_f, base_a, xi, xg, xh, fh, fl, ah, al, tiles, wide):
    to_blocks(image, xi, tiles)
    to_blocks(gradient, xg, tiles)
    to_blocks(weight, xh, tiles)
    build_weights(base_f, HALF - 1, fh, fl, wide)
    build_weights(base_a, HALF, ah, al, wide)


def forward_kernel(below, own, above, h, fh, fl, out):
    out[...] = h[...] * blur([below[...], own[...], above[...]], fh, fl)


def adjoint_kernel(below, own, above, g, ah, al, out):
    out[...] = g[...] + blur([below[...], own[...], above[...]], ah, al)


def sums_kernel(below, own, above, h, fh, fl, out):
    d = own[...]
    b = blur([below[...], d, above[...]], fh, fl)
    first = jnp.sum(d * d, axis=0, keepdims=True)
    second = jnp.sum(h[...] * b * b, axis=0, keepdims=True)
    out[...] = jnp.concatenate([first, second], axis=0)


def shrink_kernel(*refs, count, final):
    stripes, alive_ref, limits_ref, spline = refs[:count], refs[count], refs[count + 1], refs[count + 2]
    out, levels = refs[count + 3], refs[count + 4]
    alive = [alive_ref[t] for t in range(count)]
    column_cascade(stripes, alive, levels, 8)
    row_cascade(levels, spline)
    new = keep(stripes[count // 2][...], levels, [limits_ref[k] for k in range(levels.shape[0])])
    if final:
        whole, tiles = refs[count + 5], refs[count + 6]
        whole[...] = new
        from_blocks(whole, out, tiles)
    else:
        out[...] = new


def call(kernel, outs, *args, scratch=(), smem=()):
    specs = [pl.BlockSpec(memory_space=pltpu.SMEM) if n in smem else VMEM for n in range(len(args))]
    many = isinstance(outs, list)
    return pl.pallas_call(
        kernel,
        out_shape=outs,
        in_specs=specs,
        out_specs=[VMEM] * len(outs) if many else VMEM,
        scratch_shapes=list(scratch),
        compiler_params=pltpu.CompilerParams(vmem_limit_bytes=56 * 1024 * 1024),
    )(*args)


def bases(taps, wide_taps):
    rows = taps.shape[0]
    flipped = jnp.flip(taps, axis=2)
    forward = jnp.stack([jnp.pad(flipped[r], ((r, rows - r), (0, 0))) for r in range(rows)], axis=1)
    padded = jnp.pad(wide_taps, ((0, 0), (rows, rows), (0, 0)))
    adjoint = jnp.stack(
        [padded[i, 3 * rows - i : 4 * rows - i] for i in range(3 * rows)], axis=0
    )
    widen = lambda x: jnp.pad(x, ((0, 0), (0, 0), (0, BLOCK - TILE))).reshape(3 * rows, WIDTH)
    return widen(forward), widen(adjoint)


def body(image_now, gradient, hessian_weight, psf_tiles, facet_of_row, tile_slot, thresholds):
    band, columns = image_now.shape
    levels = thresholds.shape[0]
    blocks = columns // BLOCK
    count = lax.axis_size("rows") * lax.axis_size("scales")
    me = lax.axis_index("rows") * lax.axis_size("scales") + lax.axis_index("scales")

    def from_offset(x, offset):
        pairs = [(i, i - offset) for i in range(count) if 0 <= i - offset < count]
        return lax.ppermute(x, AXES, pairs)

    facet_ids = jnp.arange(tile_slot.shape[0], dtype=jnp.int32)
    slot_rows = jnp.sum(
        jnp.where(facet_of_row[:, None] == facet_ids[None, :], tile_slot[None, :], 0), axis=1
    )
    tiles_in = lax.all_gather(psf_tiles, AXES, axis=0, tiled=True)
    length = tiles_in.shape[0]
    onehot = (slot_rows[:, None] == jnp.arange(length, dtype=jnp.int32)[None, :]).astype(jnp.float32)
    flat = jnp.dot(
        onehot, tiles_in, precision=lax.Precision.HIGHEST, preferred_element_type=jnp.float32
    )
    wide_flat = jnp.concatenate([from_offset(flat, -1), flat, from_offset(flat, 1)], axis=0)
    base_f, base_a = bases(
        flat.reshape(band, TILE, TILE), wide_flat.reshape(3 * band, TILE, TILE)
    )
    plane = jax.ShapeDtypeStruct((blocks, WIDTH), jnp.float32)
    table = jax.ShapeDtypeStruct((9, WIDTH, WIDTH), jnp.bfloat16)
    tiles = pltpu.VMEM((columns // LANES * 8, LANES), jnp.float32)
    xi, xg, xh, fh, fl, ah, al = call(
        prepare_kernel,
        [plane] * 3 + [table] * 4,
        image_now, gradient, hessian_weight, base_f, base_a,
        scratch=[tiles, pltpu.VMEM((3, 2, WIDTH, LANES), jnp.float32)],
    )
    spline = spline_matrices(levels)
    reach = 2 ** (levels + 1) - 2
    side = -(-reach // band)
    offsets = list(range(-side, side + 1))
    alive = jnp.stack([((me + o >= 0) & (me + o < count)).astype(jnp.float32) for o in offsets])

    def around(x):
        return from_offset(x, -1), x, from_offset(x, 1)

    current = xi
    for sweep in range(SUBITERS):
        if sweep == 0:
            descent = xg
        else:
            pushed = call(forward_kernel, plane, *around(current - xi), xh, fh, fl)
            descent = call(adjoint_kernel, plane, *around(pushed), xg, ah, al)
        sums = call(
            sums_kernel, jax.ShapeDtypeStruct((2, WIDTH), jnp.float32), *around(descent), xh, fh, fl
        )
        totals = lax.psum(jnp.sum(sums, axis=1), AXES)
        step_size = totals[0] / totals[1]
        trial = current - step_size * descent
        stripes = [from_offset(trial, o) if o else trial for o in offsets]
        final = sweep == SUBITERS - 1
        scratch = [pltpu.VMEM((levels, blocks, WIDTH), jnp.float32)]
        if final:
            scratch += [pltpu.VMEM((blocks, WIDTH), jnp.float32), tiles]
        n = len(stripes)
        current = call(
            functools.partial(shrink_kernel, count=n, final=final),
            jax.ShapeDtypeStruct((band, columns), jnp.float32) if final else plane,
            *stripes, alive, step_size * thresholds, spline,
            scratch=scratch, smem=(n, n + 1),
        )
    return current


def solution(mesh):
    band = P(AXES, None)
    in_specs = (band, band, band, band, P(AXES), P(), P())
    return jax.shard_map(body, mesh=mesh, in_specs=in_specs, out_specs=band, check_vma=False)
```

time: 674 us -> 315 us (0.47)
  waiting for transfers between devices: 208 us -> 28.7 us
  other arithmetic: 158 us -> 5.15 us
  blocking collectives: 181 us -> 128 us
  Pallas kernels: 0 us -> 51.3 us
  local copies, waits for them, and re-layouts: 49.9 us -> 8.73 us
  starting transfers between devices: 52.9 us -> 86.3 us
  between operations: 17.6 us -> 3.3 us
    add x108 -> x0, other arithmetic: 140 us -> none  [the longest x64 81 us: forward_add_tap_row(): summed + tap_weights[:, column:column + 1] * shifted[:, column:column + c...]
    all_to_all x4 -> x0, waiting for transfers between devices: 93.5 us -> none  [the longest x2 48.6 us: body(): lax.all_to_all(upper, 'rows', split_axis=1, concat_axis=0, tiled=True)]
    all_to_all x2 -> x0, blocking collectives: 59.6 us -> none  [body(): lax.all_to_all(kept, 'rows', split_axis=0, concat_axis=1, tiled=True)]
    ppermute x14 -> x26, starting transfers between devices: 33.7 us -> 86.3 us  [from_offset(): return lax.ppermute(x, AXES, pairs)]
    pallas_call x0 -> x7, Pallas kernels: none -> 51.3 us  [call(): pl.pallas_call(kernel, out_shape=outs, in_specs=specs, out_specs=[VMEM] *...]
    reduce_scatter x2 -> x0, waiting for transfers between devices: 50.1 us -> none  [body(): lax.psum_scatter(contribution, 'scales', scatter_dimension=0, tiled=True)]
    slice x96 -> x19, local copies, waits for them, and re-layouts: 41.4 us -> 2.44 us  [the longest x17 1.27 us: bases(): flipped[r]]
    all_gather x2 -> x0, waiting for transfers between devices: 37.5 us -> none  [body(): stripe = lax.all_gather(trial, 'scales', axis=0, tiled=True)]
  transfers between devices with their start and end apart: 22 -> 26, of which waited for: 17 -> 14; matrix products, arithmetic and copies ran while one was open for 1% -> 1% of each run, Pallas kernels for 0% -> 0%
where the time goes in v1:
time: 315 us; the launch traced here: 311 us
  blocking collectives  128 us (41%)
  starting transfers between devices  86.3 us (27%)
  Pallas kernels  51.3 us (16%)
  waiting for transfers between devices  28.7 us (9%)
  local copies, waits for them, and re-layouts  8.73 us (3%)
  other arithmetic  5.15 us (2%)
  between operations  3.3 us (1%)
    ppermute x26, starting transfers between devices, from_offset(): return lax.ppermute(x, AXES, pairs)  86.3 us
    psum x2, blocking collectives, body(): totals = lax.psum(jnp.sum(sums, axis=1), AXES)  84.4 us
    pallas_call x7, Pallas kernels, call(): pl.pallas_call(kernel, out_shape=outs, in_specs=specs, out_specs=[VMEM] *...  51.3 us
    all_gather x1, blocking collectives, body(): tiles_in = lax.all_gather(psf_tiles, AXES, axis=0, tiled=True)  43.4 us
    ppermute x26, waiting for transfers between devices, from_offset(): return lax.ppermute(x, AXES, pairs)  28.7 us
  transfers between devices with their start and end apart: 26, of which 14 were waited for; matrix products, arithmetic and copies ran while one was open for 1% of the time, Pallas kernels for 0%

profile of v1, /device:TPU:1, one launch (start us, length us, event | category | flops | bytes accessed | tf_op | source)
XLA Modules:
  0.0 311.5 jit_solution(3799405523153476115)
XLA Ops:
  0.0 43.4 %all-gather = f32[32,1,256]{2,1,0:T(1,128)S(1)} all-gather(f32[1,1,256]{2,1,0:T(1,128)} %bitcast.47), channel_id=1, replica_groups=mesh['rows'=8,'scales'=4] {'rows','scales'}, dimensions={0}, use_global_device_ids=true | all-gather | bytes 33792 | tf_op jit(solution)/shard_map/all_gather | solution.py:281
  43.4 0.9 select_reduce_fusion
  44.4 2.1 collective-permute-start.1
  46.5 3.5 %collective-permute-start = (f32[8,256]{1,0:T(8,128)S(1)}, f32[8,256]{1,0:T(8,128)S(1)}, u32[]{:S(2)}, u32[]{:S(2)}) collective-permute-start(f32[8,256]{1,0:T(8,128)S(1)} %fusion), channel_id=1, source_target_pairs={{0,1},{1,2},{2,3},{3,4},{4,5},{5,6},{6,7},{7,8},{8,9},{9,10},{10,1... | collective-permute-start | bytes 24584 | tf_op jit(solution)/shard_map/ppermute | solution.py:275
  51.6 0.7 reshape.23.base_f
  52.7 0.7 reshape.25.base_a
  53.4 8.2 %shard_map.82 = (f32[256,256]{1,0:T(8,128)}, f32[256,256]{1,0:T(8,128)}, f32[256,256]{1,0:T(8,128)}, bf16[9,256,256]{2,1,0:T(8,128)(2,1)}, bf16[9,256,256]{2,1,0...) custom-call(f32[8,8192]{1,0:T(8,128)} %image.1, f32[8,8192]{1,0:T(8,128)} %gradient.1, ...), custom_call_target="tpu_custom_call" | custom-call | tf_op jit(solution)/shard_map/pallas_call | solution.py:244
  61.6 1.9 collective-permute-start.3
  63.5 3.6 %collective-permute-start.2 = (f32[256,256]{1,0:T(8,128)}, f32[256,256]{1,0:T(8,128)S(1)}, u32[]{:S(2)}, u32[]{:S(2)}) collective-permute-start(f32[256,256]{1,0:T(8,128)} %get-tuple-element.13.own.g), channel_id=1, source_target_pairs={{0,1},{1,2},{2,3},{3,4},{4,5},{5,6},{6,7},{7,8},{8,9},{9,10},{10,1... | collective-permute-start | bytes 786440 | tf_op jit(solution)/shard_map/ppermute | solution.py:275
  67.1 2.3 collective-permute-done.3.above
  69.5 1.3 collective-permute-done.2.below
  70.8 0.7 copy-done.30
  71.5 3.7 %shard_map.83 = f32[2,256]{1,0:T(2,128)} custom-call(f32[256,256]{1,0:T(8,128)} %copy-done.30, f32[256,256]{1,0:T(8,128)} %get-tuple-element.13.own.g, f32[256,256]{1,0:T(8,128)} %copy-done.28, f32[256,256]{1,0:T(8,128)} %get-tuple-element.14.h, bf16[9,256,256]{2,1,0:T(8,128)(2,1)} %get-tuple-element.15.fh, bf16[9,256,256]{2,1,0:T(8,128)(2,1)} %get-tuple-element.16.fl), custom_call_target="tpu_custom_call" | custom-call | tf_op jit(solution)/shard_map/pallas_call | solution.py:244
  75.1 0.8 reduce_sum.28
  75.9 36.3 %psum.14 = f32[2]{0:T(128)S(1)} all-reduce(f32[2]{0:T(128)S(1)} %reduce_sum.28), channel_id=1, replica_groups=mesh['rows'=8,'scales'=4] {'rows','scales'}, use_global_device_ids=true, to_apply=%region_2.3 | all-reduce | flops 2 | bytes 16 | tf_op jit(solution)/shard_map/psum | solution.py:319
  112.2 0.6 fusion.5
  114.2 1.3 collective-permute-start.11
  115.5 1.3 collective-permute-start.10
  116.8 1.3 collective-permute-start.9
  118.1 3.4 %collective-permute-start.8 = (f32[256,256]{1,0:T(8,128)S(1)}, f32[256,256]{1,0:T(8,128)S(1)}, u32[]{:S(2)}, u32[]{:S(2)}) collective-permute-start(f32[256,256]{1,0:T(8,128)S(1)} %multiply_subtract_fusion.1.refs_4_), channel_id=1, source_target_pairs={{1,0},{2,1},{3,2},{4,3},{5,4},{6,5},{7,6},{8,7},{9,8},{10,9},{11,1... | collective-permute-start | bytes 786440 | tf_op jit(solution)/shard_map/ppermute | solution.py:275
  121.5 4.4 %collective-permute-start.7 = (f32[256,256]{1,0:T(8,128)S(1)}, f32[256,256]{1,0:T(8,128)S(1)}, u32[]{:S(2)}, u32[]{:S(2)}) collective-permute-start(f32[256,256]{1,0:T(8,128)S(1)} %multiply_subtract_fusion.1.refs_4_), channel_id=1, source_target_pairs={{0,1},{1,2},{2,3},{3,4},{4,5},{5,6},{6,7},{7,8},{8,9},{9,10},{10,1... | collective-permute-start | bytes 786440 | tf_op jit(solution)/shard_map/ppermute | solution.py:275
  125.9 4.6 %collective-permute-start.6 = (f32[256,256]{1,0:T(8,128)S(1)}, f32[256,256]{1,0:T(8,128)S(1)}, u32[]{:S(2)}, u32[]{:S(2)}) collective-permute-start(f32[256,256]{1,0:T(8,128)S(1)} %multiply_subtract_fusion.1.refs_4_), channel_id=1, source_target_pairs={{0,2},{1,3},{2,4},{3,5},{4,6},{5,7},{6,8},{7,9},{8,10},{9,11},{10,... | collective-permute-start | bytes 786440 | tf_op jit(solution)/shard_map/ppermute | solution.py:275
  130.6 1.3 collective-permute-done.10.refs_7_
  131.9 1.8 collective-permute-start.5
  133.7 9.7 %collective-permute-start.4 = (f32[256,256]{1,0:T(8,128)S(1)}, f32[256,256]{1,0:T(8,128)S(1)}, u32[]{:S(2)}, u32[]{:S(2)}) collective-permute-start(f32[256,256]{1,0:T(8,128)S(1)} %multiply_subtract_fusion.1.refs_4_), channel_id=1, source_target_pairs={{0,4},{1,5},{2,6},{3,7},{4,8},{5,9},{6,10},{7,11},{8,12},{9,13},{1... | collective-permute-start | bytes 786440 | tf_op jit(solution)/shard_map/ppermute | solution.py:275
  144.1 0.6 broadcast_multiply_fusion.1.refs_10_
  144.7 0.7 collective-permute-done.6.refs_2_
  145.4 3.8 %collective-permute-done.4.refs_0_ = f32[256,256]{1,0:T(8,128)S(1)} collective-permute-done((f32[256,256]{1,0:T(8,128)S(1)}, f32[256,256]{1,0:T(8,128)S(1)}, u32[]{:S(2)}, u32[]{:S(2)}) %collective-permute-start.4) | collective-permute-done | bytes 262176 | tf_op jit(solution)/shard_map/ppermute | solution.py:275
  149.2 0.7 copy-done.18
  149.9 14.1 %shard_map.84 = f32[256,256]{1,0:T(8,128)} custom-call(f32[256,256]{1,0:T(8,128)} %copy-done.18, f32[256,256]{1,0:T(8,128)} %copy-done.17, f32[256,256]{1,0:T(8,128)} %copy-done.16, f32[256,256]{1,0:T(8,128)} %copy-done.15, f32[256,256]{1,0:T(8,128)} %copy-done.5, f32[256,256]{1,0:T(8,128)} %copy-done.14, f32[256,256]{1,0:T(8,128)} %copy-done.13, ...), custom_call_target="tpu_custom_call" | custom-call | tf_op jit(solution)/shard_map/pallas_call | solution.py:244
  164.0 1.0 sub.10.own
  165.0 1.9 collective-permute-start.13
  167.0 3.6 %collective-permute-start.12 = (f32[256,256]{1,0:T(8,128)S(1)}, f32[256,256]{1,0:T(8,128)S(1)}, u32[]{:S(2)}, u32[]{:S(2)}) collective-permute-start(f32[256,256]{1,0:T(8,128)S(1)} %sub.10.own), channel_id=1, source_target_pairs={{0,1},{1,2},{2,3},{3,4},{4,5},{5,6},{6,7},{7,8},{8,9},{9,10},{10,1... | collective-permute-start | bytes 786440 | tf_op jit(solution)/shard_map/ppermute | solution.py:275
  170.6 2.1 collective-permute-done.13.above
  172.7 2.5 collective-permute-done.12.below
  175.2 0.7 copy-done.10
  175.9 3.7 %shard_map.85.own = f32[256,256]{1,0:T(8,128)} custom-call(f32[256,256]{1,0:T(8,128)} %copy-done.10, f32[256,256]{1,0:T(8,128)} %copy-done.3, f32[256,256]{1,0:T(8,128)} %copy-done.9, f32[256,256]{1,0:T(8,128)} %get-tuple-element.14.h, bf16[9,256,256]{2,1,0:T(8,128)(2,1)} %get-tuple-element.15.fh, bf16[9,256,256]{2,1,0:T(8,128)(2,1)} %get-tuple-element.16.fl), custom_call_target="tpu_custom_call" | custom-call | tf_op jit(solution)/shard_map/pallas_call | solution.py:244
  179.6 1.9 collective-permute-start.15
  181.6 4.6 %collective-permute-start.14 = (f32[256,256]{1,0:T(8,128)}, f32[256,256]{1,0:T(8,128)S(1)}, u32[]{:S(2)}, u32[]{:S(2)}) collective-permute-start(f32[256,256]{1,0:T(8,128)} %shard_map.85.own), channel_id=1, source_target_pairs={{0,1},{1,2},{2,3},{3,4},{4,5},{5,6},{6,7},{7,8},{8,9},{9,10},{10,1... | collective-permute-start | bytes 786440 | tf_op jit(solution)/shard_map/ppermute | solution.py:275
  186.1 2.1 collective-permute-done.15.above
  188.3 2.3 collective-permute-done.14.below
  190.6 0.7 copy-done.8
  191.3 3.7 %shard_map.86.own = f32[256,256]{1,0:T(8,128)} custom-call(f32[256,256]{1,0:T(8,128)} %copy-done.8, f32[256,256]{1,0:T(8,128)} %shard_map.85.own, f32[256,256]{1,0:T(8,128)} %copy-done.7, f32[256,256]{1,0:T(8,128)} %get-tuple-element.13.own.g, bf16[9,256,256]{2,1,0:T(8,128)(2,1)} %get-tuple-element.17.ah, bf16[9,256,256]{2,1,0:T(8,128)(2,1)} %get-tuple-element.18.al), custom_call_target="tpu_custom_call" | custom-call | tf_op jit(solution)/shard_map/pallas_call | solution.py:244
  195.0 2.0 collective-permute-start.17
  197.1 4.3 %collective-permute-start.16 = (f32[256,256]{1,0:T(8,128)}, f32[256,256]{1,0:T(8,128)S(1)}, u32[]{:S(2)}, u32[]{:S(2)}) collective-permute-start(f32[256,256]{1,0:T(8,128)} %shard_map.86.own), channel_id=1, source_target_pairs={{0,1},{1,2},{2,3},{3,4},{4,5},{5,6},{6,7},{7,8},{8,9},{9,10},{10,1... | collective-permute-start | bytes 786440 | tf_op jit(solution)/shard_map/ppermute | solution.py:275
  201.3 2.3 collective-permute-done.17.above
  203.7 2.3 collective-permute-done.16.below
  206.0 0.7 copy-done.29
  206.7 3.6 %shard_map.87 = f32[2,256]{1,0:T(2,128)} custom-call(f32[256,256]{1,0:T(8,128)} %copy-done.29, f32[256,256]{1,0:T(8,128)} %shard_map.86.own, f32[256,256]{1,0:T(8,128)} %copy-done.27, f32[256,256]{1,0:T(8,128)} %get-tuple-element.14.h, bf16[9,256,256]{2,1,0:T(8,128)(2,1)} %get-tuple-element.15.fh, bf16[9,256,256]{2,1,0:T(8,128)(2,1)} %get-tuple-element.16.fl), custom_call_target="tpu_custom_call" | custom-call | tf_op jit(solution)/shard_map/pallas_call | solution.py:244
  210.3 0.8 reduce_sum.29
  211.1 48.1 %psum.15 = f32[2]{0:T(128)S(1)} all-reduce(f32[2]{0:T(128)S(1)} %reduce_sum.29), channel_id=1, replica_groups=mesh['rows'=8,'scales'=4] {'rows','scales'}, use_global_device_ids=true, to_apply=%region_4.5 | all-reduce | flops 2 | bytes 16 | tf_op jit(solution)/shard_map/psum | solution.py:319
  259.2 0.6 fusion.4
  261.1 1.3 collective-permute-start.25
  262.4 1.3 collective-permute-start.24
  263.7 1.3 collective-permute-start.23
  265.0 3.4 %collective-permute-start.22 = (f32[256,256]{1,0:T(8,128)S(1)}, f32[256,256]{1,0:T(8,128)S(1)}, u32[]{:S(2)}, u32[]{:S(2)}) collective-permute-start(f32[256,256]{1,0:T(8,128)S(1)} %multiply_subtract_fusion.refs_4_), channel_id=1, source_target_pairs={{1,0},{2,1},{3,2},{4,3},{5,4},{6,5},{7,6},{8,7},{9,8},{10,9},{11,1... | collective-permute-start | bytes 786440 | tf_op jit(solution)/shard_map/ppermute | solution.py:275
  268.4 4.4 %collective-permute-start.21 = (f32[256,256]{1,0:T(8,128)S(1)}, f32[256,256]{1,0:T(8,128)S(1)}, u32[]{:S(2)}, u32[]{:S(2)}) collective-permute-start(f32[256,256]{1,0:T(8,128)S(1)} %multiply_subtract_fusion.refs_4_), channel_id=1, source_target_pairs={{0,1},{1,2},{2,3},{3,4},{4,5},{5,6},{6,7},{7,8},{8,9},{9,10},{10,1... | collective-permute-start | bytes 786440 | tf_op jit(solution)/shard_map/ppermute | solution.py:275
  272.9 4.6 %collective-permute-start.20 = (f32[256,256]{1,0:T(8,128)S(1)}, f32[256,256]{1,0:T(8,128)S(1)}, u32[]{:S(2)}, u32[]{:S(2)}) collective-permute-start(f32[256,256]{1,0:T(8,128)S(1)} %multiply_subtract_fusion.refs_4_), channel_id=1, source_target_pairs={{0,2},{1,3},{2,4},{3,5},{4,6},{5,7},{6,8},{7,9},{8,10},{9,11},{10,... | collective-permute-start | bytes 786440 | tf_op jit(solution)/shard_map/ppermute | solution.py:275
  277.9 2.8 collective-permute-start.19
  280.7 9.9 %collective-permute-start.18 = (f32[256,256]{1,0:T(8,128)S(1)}, f32[256,256]{1,0:T(8,128)S(1)}, u32[]{:S(2)}, u32[]{:S(2)}) collective-permute-start(f32[256,256]{1,0:T(8,128)S(1)} %multiply_subtract_fusion.refs_4_), channel_id=1, source_target_pairs={{0,4},{1,5},{2,6},{3,7},{4,8},{5,9},{6,10},{7,11},{8,12},{9,13},{1... | collective-permute-start | bytes 786440 | tf_op jit(solution)/shard_map/ppermute | solution.py:275
  291.2 1.0 collective-permute-done.20.refs_2_
  292.2 4.2 %collective-permute-done.18.refs_0_ = f32[256,256]{1,0:T(8,128)S(1)} collective-permute-done((f32[256,256]{1,0:T(8,128)S(1)}, f32[256,256]{1,0:T(8,128)S(1)}, u32[]{:S(2)}, u32[]{:S(2)}) %collective-permute-start.18) | collective-permute-done | bytes 262176 | tf_op jit(solution)/shard_map/ppermute | solution.py:275
  296.5 0.7 copy-done.26
  297.2 14.3 %shard_map.88 = f32[8,8192]{1,0:T(8,128)} custom-call(f32[256,256]{1,0:T(8,128)} %copy-done.26, f32[256,256]{1,0:T(8,128)} %copy-done.25, f32[256,256]{1,0:T(8,128)} %copy-done.24, f32[256,256]{1,0:T(8,128)} %copy-done.23, f32[256,256]{1,0:T(8,128)} %copy-done.6, f32[256,256]{1,0:T(8,128)} %copy-done.22, f32[256,256]{1,0:T(8,128)} %copy-done.21, ...), custom_call_target="tpu_custom_call" | custom-call | tf_op jit(solution)/shard_map/pallas_call | solution.py:244
  (131 shorter events, 3.7 us)
Async XLA Ops:
  44.4 7.8 %collective-permute-start.1 = (f32[8,256]{1,0:T(8,128)S(1)}, f32[8,256]{1,0:T(8,128)S(1)}, u32[]{:S(2)}, u32[]{:S(2)}) collective-permute-start(f32[8,256]{1,0:T(8,128)S(1)} %fusion), channel_id=1, source_target_pairs={{1,0},{2,1},{3,2},{4,3},{5,4},{6,5},{7,6},{8,7},{9,8},{10,9},{11,1... | collective-permute-start | bytes 24584 | tf_op jit(solution)/shard_map/ppermute | solution.py:275
  46.5 5.8 %collective-permute-start = (f32[8,256]{1,0:T(8,128)S(1)}, f32[8,256]{1,0:T(8,128)S(1)}, u32[]{:S(2)}, u32[]{:S(2)}) collective-permute-start(f32[8,256]{1,0:T(8,128)S(1)} %fusion), channel_id=1, source_target_pairs={{0,1},{1,2},{2,3},{3,4},{4,5},{5,6},{6,7},{7,8},{8,9},{9,10},{10,1... | collective-permute-start | bytes 24584 | tf_op jit(solution)/shard_map/ppermute | solution.py:275
  61.6 7.9 %collective-permute-start.3 = (f32[256,256]{1,0:T(8,128)}, f32[256,256]{1,0:T(8,128)S(1)}, u32[]{:S(2)}, u32[]{:S(2)}) collective-permute-start(f32[256,256]{1,0:T(8,128)} %get-tuple-element.13.own.g), channel_id=1, source_target_pairs={{1,0},{2,1},{3,2},{4,3},{5,4},{6,5},{7,6},{8,7},{9,8},{10,9},{11,1... | collective-permute-start | bytes 786440 | tf_op jit(solution)/shard_map/ppermute | solution.py:275
  63.5 7.3 %collective-permute-start.2 = (f32[256,256]{1,0:T(8,128)}, f32[256,256]{1,0:T(8,128)S(1)}, u32[]{:S(2)}, u32[]{:S(2)}) collective-permute-start(f32[256,256]{1,0:T(8,128)} %get-tuple-element.13.own.g), channel_id=1, source_target_pairs={{0,1},{1,2},{2,3},{3,4},{4,5},{5,6},{6,7},{7,8},{8,9},{9,10},{10,1... | collective-permute-start | bytes 786440 | tf_op jit(solution)/shard_map/ppermute | solution.py:275
  69.5 1.3 copy-start.28
  70.7 0.7 copy-start.30
  71.4 42.6 %copy-start = (f32[256,256]{1,0:T(8,128)S(1)}, f32[256,256]{1,0:T(8,128)}, u32[]{:S(2)}) copy-start(f32[256,256]{1,0:T(8,128)} %get-tuple-element.13.own.g) | copy-start | bytes 786436
  71.4 42.7 %copy-start.4 = (f32[256,256]{1,0:T(8,128)S(1)}, f32[256,256]{1,0:T(8,128)}, u32[]{:S(2)}) copy-start(f32[256,256]{1,0:T(8,128)} %get-tuple-element.12) | copy-start | bytes 786436
  71.5 72.6 %copy-start.31 = (f32[4]{0:T(128)S(1)}, f32[4]{0:T(128)}, u32[]{:S(2)}) copy-start(f32[4]{0:T(128)} %param.14) | copy-start | bytes 52
  114.2 35.0 %copy-start.5 = (f32[256,256]{1,0:T(8,128)}, f32[256,256]{1,0:T(8,128)S(1)}, u32[]{:S(2)}) copy-start(f32[256,256]{1,0:T(8,128)S(1)} %multiply_subtract_fusion.1.refs_4_) | copy-start | bytes 786436
  114.2 11.7 %collective-permute-start.11 = (f32[256,256]{1,0:T(8,128)S(1)}, f32[256,256]{1,0:T(8,128)S(1)}, u32[]{:S(2)}, u32[]{:S(2)}) collective-permute-start(f32[256,256]{1,0:T(8,128)S(1)} %multiply_subtract_fusion.1.refs_4_), channel_id=1, source_target_pairs={{4,0},{5,1},{6,2},{7,3},{8,4},{9,5},{10,6},{11,7},{12,8},{13,9},{1... | collective-permute-start | bytes 786440 | tf_op jit(solution)/shard_map/ppermute | solution.py:275
  115.5 16.4 %collective-permute-start.10 = (f32[256,256]{1,0:T(8,128)S(1)}, f32[256,256]{1,0:T(8,128)S(1)}, u32[]{:S(2)}, u32[]{:S(2)}) collective-permute-start(f32[256,256]{1,0:T(8,128)S(1)} %multiply_subtract_fusion.1.refs_4_), channel_id=1, source_target_pairs={{3,0},{4,1},{5,2},{6,3},{7,4},{8,5},{9,6},{10,7},{11,8},{12,9},{13... | collective-permute-start | bytes 786440 | tf_op jit(solution)/shard_map/ppermute | solution.py:275
  116.8 16.9 %collective-permute-start.9 = (f32[256,256]{1,0:T(8,128)S(1)}, f32[256,256]{1,0:T(8,128)S(1)}, u32[]{:S(2)}, u32[]{:S(2)}) collective-permute-start(f32[256,256]{1,0:T(8,128)S(1)} %multiply_subtract_fusion.1.refs_4_), channel_id=1, source_target_pairs={{2,0},{3,1},{4,2},{5,3},{6,4},{7,5},{8,6},{9,7},{10,8},{11,9},{12,... | collective-permute-start | bytes 786440 | tf_op jit(solution)/shard_map/ppermute | solution.py:275
  118.1 26.6 %collective-permute-start.8 = (f32[256,256]{1,0:T(8,128)S(1)}, f32[256,256]{1,0:T(8,128)S(1)}, u32[]{:S(2)}, u32[]{:S(2)}) collective-permute-start(f32[256,256]{1,0:T(8,128)S(1)} %multiply_subtract_fusion.1.refs_4_), channel_id=1, source_target_pairs={{1,0},{2,1},{3,2},{4,3},{5,4},{6,5},{7,6},{8,7},{9,8},{10,9},{11,1... | collective-permute-start | bytes 786440 | tf_op jit(solution)/shard_map/ppermute | solution.py:275
  121.5 23.2 %collective-permute-start.7 = (f32[256,256]{1,0:T(8,128)S(1)}, f32[256,256]{1,0:T(8,128)S(1)}, u32[]{:S(2)}, u32[]{:S(2)}) collective-permute-start(f32[256,256]{1,0:T(8,128)S(1)} %multiply_subtract_fusion.1.refs_4_), channel_id=1, source_target_pairs={{0,1},{1,2},{2,3},{3,4},{4,5},{5,6},{6,7},{7,8},{8,9},{9,10},{10,1... | collective-permute-start | bytes 786440 | tf_op jit(solution)/shard_map/ppermute | solution.py:275
  125.9 23.3 %copy-start.11 = (f32[256,256]{1,0:T(8,128)}, f32[256,256]{1,0:T(8,128)S(1)}, u32[]{:S(2)}) copy-start(f32[256,256]{1,0:T(8,128)S(1)} %collective-permute-done.11.refs_8_) | copy-start | bytes 786436
  125.9 19.4 %collective-permute-start.6 = (f32[256,256]{1,0:T(8,128)S(1)}, f32[256,256]{1,0:T(8,128)S(1)}, u32[]{:S(2)}, u32[]{:S(2)}) collective-permute-start(f32[256,256]{1,0:T(8,128)S(1)} %multiply_subtract_fusion.1.refs_4_), channel_id=1, source_target_pairs={{0,2},{1,3},{2,4},{3,5},{4,6},{5,7},{6,8},{7,9},{8,10},{9,11},{10,... | collective-permute-start | bytes 786440 | tf_op jit(solution)/shard_map/ppermute | solution.py:275
  131.9 17.3 %copy-start.12 = (f32[256,256]{1,0:T(8,128)}, f32[256,256]{1,0:T(8,128)S(1)}, u32[]{:S(2)}) copy-start(f32[256,256]{1,0:T(8,128)S(1)} %collective-permute-done.10.refs_7_) | copy-start | bytes 786436
  131.9 13.4 %collective-permute-start.5 = (f32[256,256]{1,0:T(8,128)S(1)}, f32[256,256]{1,0:T(8,128)S(1)}, u32[]{:S(2)}, u32[]{:S(2)}) collective-permute-start(f32[256,256]{1,0:T(8,128)S(1)} %multiply_subtract_fusion.1.refs_4_), channel_id=1, source_target_pairs={{0,3},{1,4},{2,5},{3,6},{4,7},{5,8},{6,9},{7,10},{8,11},{9,12},{10... | collective-permute-start | bytes 786440 | tf_op jit(solution)/shard_map/ppermute | solution.py:275
  133.7 15.5 %copy-start.13 = (f32[256,256]{1,0:T(8,128)}, f32[256,256]{1,0:T(8,128)S(1)}, u32[]{:S(2)}) copy-start(f32[256,256]{1,0:T(8,128)S(1)} %collective-permute-done.9.refs_6_) | copy-start | bytes 786436
  133.7 15.4 %collective-permute-start.4 = (f32[256,256]{1,0:T(8,128)S(1)}, f32[256,256]{1,0:T(8,128)S(1)}, u32[]{:S(2)}, u32[]{:S(2)}) collective-permute-start(f32[256,256]{1,0:T(8,128)S(1)} %multiply_subtract_fusion.1.refs_4_), channel_id=1, source_target_pairs={{0,4},{1,5},{2,6},{3,7},{4,8},{5,9},{6,10},{7,11},{8,12},{9,13},{1... | collective-permute-start | bytes 786440 | tf_op jit(solution)/shard_map/ppermute | solution.py:275
  144.7 4.5 %copy-start.14 = (f32[256,256]{1,0:T(8,128)}, f32[256,256]{1,0:T(8,128)S(1)}, u32[]{:S(2)}) copy-start(f32[256,256]{1,0:T(8,128)S(1)} %collective-permute-done.8.refs_5_) | copy-start | bytes 786436
  144.7 4.5 %copy-start.15 = (f32[256,256]{1,0:T(8,128)}, f32[256,256]{1,0:T(8,128)S(1)}, u32[]{:S(2)}) copy-start(f32[256,256]{1,0:T(8,128)S(1)} %collective-permute-done.7.refs_3_) | copy-start | bytes 786436
  145.4 3.8 %copy-start.16 = (f32[256,256]{1,0:T(8,128)}, f32[256,256]{1,0:T(8,128)S(1)}, u32[]{:S(2)}) copy-start(f32[256,256]{1,0:T(8,128)S(1)} %collective-permute-done.6.refs_2_) | copy-start | bytes 786436
  145.4 3.8 %copy-start.17 = (f32[256,256]{1,0:T(8,128)}, f32[256,256]{1,0:T(8,128)S(1)}, u32[]{:S(2)}) copy-start(f32[256,256]{1,0:T(8,128)S(1)} %collective-permute-done.5.refs_1_) | copy-start | bytes 786436
  149.2 0.7 copy-start.18
  165.0 10.2 %copy-start.3 = (f32[256,256]{1,0:T(8,128)}, f32[256,256]{1,0:T(8,128)S(1)}, u32[]{:S(2)}) copy-start(f32[256,256]{1,0:T(8,128)S(1)} %sub.10.own) | copy-start | bytes 786436
  165.0 7.7 %collective-permute-start.13 = (f32[256,256]{1,0:T(8,128)S(1)}, f32[256,256]{1,0:T(8,128)S(1)}, u32[]{:S(2)}, u32[]{:S(2)}) collective-permute-start(f32[256,256]{1,0:T(8,128)S(1)} %sub.10.own), channel_id=1, source_target_pairs={{1,0},{2,1},{3,2},{4,3},{5,4},{6,5},{7,6},{8,7},{9,8},{10,9},{11,1... | collective-permute-start | bytes 786440 | tf_op jit(solution)/shard_map/ppermute | solution.py:275
  167.0 8.2 %collective-permute-start.12 = (f32[256,256]{1,0:T(8,128)S(1)}, f32[256,256]{1,0:T(8,128)S(1)}, u32[]{:S(2)}, u32[]{:S(2)}) collective-permute-start(f32[256,256]{1,0:T(8,128)S(1)} %sub.10.own), channel_id=1, source_target_pairs={{0,1},{1,2},{2,3},{3,4},{4,5},{5,6},{6,7},{7,8},{8,9},{9,10},{10,1... | collective-permute-start | bytes 786440 | tf_op jit(solution)/shard_map/ppermute | solution.py:275
  172.7 2.5 copy-start.9
  175.2 0.7 copy-start.10
  179.6 8.6 %collective-permute-start.15 = (f32[256,256]{1,0:T(8,128)}, f32[256,256]{1,0:T(8,128)S(1)}, u32[]{:S(2)}, u32[]{:S(2)}) collective-permute-start(f32[256,256]{1,0:T(8,128)} %shard_map.85.own), channel_id=1, source_target_pairs={{1,0},{2,1},{3,2},{4,3},{5,4},{6,5},{7,6},{8,7},{9,8},{10,9},{11,1... | collective-permute-start | bytes 786440 | tf_op jit(solution)/shard_map/ppermute | solution.py:275
  181.6 9.0 %collective-permute-start.14 = (f32[256,256]{1,0:T(8,128)}, f32[256,256]{1,0:T(8,128)S(1)}, u32[]{:S(2)}, u32[]{:S(2)}) collective-permute-start(f32[256,256]{1,0:T(8,128)} %shard_map.85.own), channel_id=1, source_target_pairs={{0,1},{1,2},{2,3},{3,4},{4,5},{5,6},{6,7},{7,8},{8,9},{9,10},{10,1... | collective-permute-start | bytes 786440 | tf_op jit(solution)/shard_map/ppermute | solution.py:275
  188.3 2.3 copy-start.7
  190.6 0.7 copy-start.8
  195.0 66.0 %copy-start.1 = (f32[256,256]{1,0:T(8,128)S(1)}, f32[256,256]{1,0:T(8,128)}, u32[]{:S(2)}) copy-start(f32[256,256]{1,0:T(8,128)} %shard_map.86.own) | copy-start | bytes 786436
  195.0 66.0 %copy-start.2 = (f32[256,256]{1,0:T(8,128)S(1)}, f32[256,256]{1,0:T(8,128)}, u32[]{:S(2)}) copy-start(f32[256,256]{1,0:T(8,128)} %shard_map.84) | copy-start | bytes 786436
  195.0 8.7 %collective-permute-start.17 = (f32[256,256]{1,0:T(8,128)}, f32[256,256]{1,0:T(8,128)S(1)}, u32[]{:S(2)}, u32[]{:S(2)}) collective-permute-start(f32[256,256]{1,0:T(8,128)} %shard_map.86.own), channel_id=1, source_target_pairs={{1,0},{2,1},{3,2},{4,3},{5,4},{6,5},{7,6},{8,7},{9,8},{10,9},{11,1... | collective-permute-start | bytes 786440 | tf_op jit(solution)/shard_map/ppermute | solution.py:275
  197.1 8.9 %collective-permute-start.16 = (f32[256,256]{1,0:T(8,128)}, f32[256,256]{1,0:T(8,128)S(1)}, u32[]{:S(2)}, u32[]{:S(2)}) collective-permute-start(f32[256,256]{1,0:T(8,128)} %shard_map.86.own), channel_id=1, source_target_pairs={{0,1},{1,2},{2,3},{3,4},{4,5},{5,6},{6,7},{7,8},{8,9},{9,10},{10,1... | collective-permute-start | bytes 786440 | tf_op jit(solution)/shard_map/ppermute | solution.py:275
  203.7 2.3 copy-start.27
  206.0 0.7 copy-start.29
  261.1 35.3 %copy-start.6 = (f32[256,256]{1,0:T(8,128)}, f32[256,256]{1,0:T(8,128)S(1)}, u32[]{:S(2)}) copy-start(f32[256,256]{1,0:T(8,128)S(1)} %multiply_subtract_fusion.refs_4_) | copy-start | bytes 786436
  261.1 11.7 %collective-permute-start.25 = (f32[256,256]{1,0:T(8,128)S(1)}, f32[256,256]{1,0:T(8,128)S(1)}, u32[]{:S(2)}, u32[]{:S(2)}) collective-permute-start(f32[256,256]{1,0:T(8,128)S(1)} %multiply_subtract_fusion.refs_4_), channel_id=1, source_target_pairs={{4,0},{5,1},{6,2},{7,3},{8,4},{9,5},{10,6},{11,7},{12,8},{13,9},{1... | collective-permute-start | bytes 786440 | tf_op jit(solution)/shard_map/ppermute | solution.py:275
  262.4 15.5 %collective-permute-start.24 = (f32[256,256]{1,0:T(8,128)S(1)}, f32[256,256]{1,0:T(8,128)S(1)}, u32[]{:S(2)}, u32[]{:S(2)}) collective-permute-start(f32[256,256]{1,0:T(8,128)S(1)} %multiply_subtract_fusion.refs_4_), channel_id=1, source_target_pairs={{3,0},{4,1},{5,2},{6,3},{7,4},{8,5},{9,6},{10,7},{11,8},{12,9},{13... | collective-permute-start | bytes 786440 | tf_op jit(solution)/shard_map/ppermute | solution.py:275
  263.7 16.9 %collective-permute-start.23 = (f32[256,256]{1,0:T(8,128)S(1)}, f32[256,256]{1,0:T(8,128)S(1)}, u32[]{:S(2)}, u32[]{:S(2)}) collective-permute-start(f32[256,256]{1,0:T(8,128)S(1)} %multiply_subtract_fusion.refs_4_), channel_id=1, source_target_pairs={{2,0},{3,1},{4,2},{5,3},{6,4},{7,5},{8,6},{9,7},{10,8},{11,9},{12,... | collective-permute-start | bytes 786440 | tf_op jit(solution)/shard_map/ppermute | solution.py:275
  265.0 26.2 %collective-permute-start.22 = (f32[256,256]{1,0:T(8,128)S(1)}, f32[256,256]{1,0:T(8,128)S(1)}, u32[]{:S(2)}, u32[]{:S(2)}) collective-permute-start(f32[256,256]{1,0:T(8,128)S(1)} %multiply_subtract_fusion.refs_4_), channel_id=1, source_target_pairs={{1,0},{2,1},{3,2},{4,3},{5,4},{6,5},{7,6},{8,7},{9,8},{10,9},{11,1... | collective-permute-start | bytes 786440 | tf_op jit(solution)/shard_map/ppermute | solution.py:275
  268.4 22.8 %collective-permute-start.21 = (f32[256,256]{1,0:T(8,128)S(1)}, f32[256,256]{1,0:T(8,128)S(1)}, u32[]{:S(2)}, u32[]{:S(2)}) collective-permute-start(f32[256,256]{1,0:T(8,128)S(1)} %multiply_subtract_fusion.refs_4_), channel_id=1, source_target_pairs={{0,1},{1,2},{2,3},{3,4},{4,5},{5,6},{6,7},{7,8},{8,9},{9,10},{10,1... | collective-permute-start | bytes 786440 | tf_op jit(solution)/shard_map/ppermute | solution.py:275
  272.8 23.6 %copy-start.19 = (f32[256,256]{1,0:T(8,128)}, f32[256,256]{1,0:T(8,128)S(1)}, u32[]{:S(2)}) copy-start(f32[256,256]{1,0:T(8,128)S(1)} %collective-permute-done.25.refs_8_) | copy-start | bytes 786436
  272.9 19.3 %collective-permute-start.20 = (f32[256,256]{1,0:T(8,128)S(1)}, f32[256,256]{1,0:T(8,128)S(1)}, u32[]{:S(2)}, u32[]{:S(2)}) collective-permute-start(f32[256,256]{1,0:T(8,128)S(1)} %multiply_subtract_fusion.refs_4_), channel_id=1, source_target_pairs={{0,2},{1,3},{2,4},{3,5},{4,6},{5,7},{6,8},{7,9},{8,10},{9,11},{10,... | collective-permute-start | bytes 786440 | tf_op jit(solution)/shard_map/ppermute | solution.py:275
  277.9 18.5 %copy-start.20 = (f32[256,256]{1,0:T(8,128)}, f32[256,256]{1,0:T(8,128)S(1)}, u32[]{:S(2)}) copy-start(f32[256,256]{1,0:T(8,128)S(1)} %collective-permute-done.24.refs_7_) | copy-start | bytes 786436
  277.9 14.3 %collective-permute-start.19 = (f32[256,256]{1,0:T(8,128)S(1)}, f32[256,256]{1,0:T(8,128)S(1)}, u32[]{:S(2)}, u32[]{:S(2)}) collective-permute-start(f32[256,256]{1,0:T(8,128)S(1)} %multiply_subtract_fusion.refs_4_), channel_id=1, source_target_pairs={{0,3},{1,4},{2,5},{3,6},{4,7},{5,8},{6,9},{7,10},{8,11},{9,12},{10... | collective-permute-start | bytes 786440 | tf_op jit(solution)/shard_map/ppermute | solution.py:275
  280.7 15.8 %copy-start.21 = (f32[256,256]{1,0:T(8,128)}, f32[256,256]{1,0:T(8,128)S(1)}, u32[]{:S(2)}) copy-start(f32[256,256]{1,0:T(8,128)S(1)} %collective-permute-done.23.refs_6_) | copy-start | bytes 786436
  280.7 15.7 %collective-permute-start.18 = (f32[256,256]{1,0:T(8,128)S(1)}, f32[256,256]{1,0:T(8,128)S(1)}, u32[]{:S(2)}, u32[]{:S(2)}) collective-permute-start(f32[256,256]{1,0:T(8,128)S(1)} %multiply_subtract_fusion.refs_4_), channel_id=1, source_target_pairs={{0,4},{1,5},{2,6},{3,7},{4,8},{5,9},{6,10},{7,11},{8,12},{9,13},{1... | collective-permute-start | bytes 786440 | tf_op jit(solution)/shard_map/ppermute | solution.py:275
  291.2 5.3 %copy-start.22 = (f32[256,256]{1,0:T(8,128)}, f32[256,256]{1,0:T(8,128)S(1)}, u32[]{:S(2)}) copy-start(f32[256,256]{1,0:T(8,128)S(1)} %collective-permute-done.22.refs_5_) | copy-start | bytes 786436
  291.2 5.3 %copy-start.23 = (f32[256,256]{1,0:T(8,128)}, f32[256,256]{1,0:T(8,128)S(1)}, u32[]{:S(2)}) copy-start(f32[256,256]{1,0:T(8,128)S(1)} %collective-permute-done.21.refs_3_) | copy-start | bytes 786436
  292.2 4.3 %copy-start.24 = (f32[256,256]{1,0:T(8,128)}, f32[256,256]{1,0:T(8,128)S(1)}, u32[]{:S(2)}) copy-start(f32[256,256]{1,0:T(8,128)S(1)} %collective-permute-done.20.refs_2_) | copy-start | bytes 786436
  292.2 4.3 %copy-start.25 = (f32[256,256]{1,0:T(8,128)}, f32[256,256]{1,0:T(8,128)S(1)}, u32[]{:S(2)}) copy-start(f32[256,256]{1,0:T(8,128)S(1)} %collective-permute-done.19.refs_1_) | copy-start | bytes 786436
  296.5 0.7 copy-start.26

commit v2 on v1

--- a/solution.py
+++ b/solution.py
@@ -57,14 +57,16 @@
 
 
 def blur(stripes, high_ref, low_ref):
+    parts = [halves(x) for x in stripes]
     total = None
-    for t, x in enumerate(stripes):
-        for s in (-1, 0, 1):
-            high, low = halves(block_shift(x, s))
-            n = t * 3 + s + 1
-            w = high_ref[n]
-            part = dot(high, w) + dot(low, w) + dot(high, low_ref[n])
-            total = part if total is None else total + part
+    for s in (-1, 0, 1):
+        here = None
+        for t, (high, low) in enumerate(parts):
+            w = high_ref[t * 3 + s + 1]
+            part = dot(high, w) + dot(low, w) + dot(high, low_ref[t * 3 + s + 1])
+            here = part if here is None else here + part
+        here = block_shift(here, s)
+        total = here if total is None else total + here
     return total
 
 
@@ -173,12 +175,11 @@
     for level in range(levels):
 
         def one(k, carry):
-            x = levels_ref[k]
+            high, low = halves(levels_ref[k])
             total = None
             for s in (-1, 0, 1):
-                high, low = halves(block_shift(x, s))
                 w = spline_ref[level * 3 + s + 1]
-                part = dot(high, w) + dot(low, w)
+                part = block_shift(dot(high, w) + dot(low, w), s)
                 total = part if total is None else total + part
             levels_ref[k] = total
             return carry
@@ -199,139 +200,224 @@
     return total + smooth
 
 
-def prepare_kernel(image, gradient, weight, base_f, base_a, xi, xg, xh, fh, fl, ah, al, tiles, wide):
+def build_bases(taps, flipped, forward, adjoint):
+    lane = lax.broadcasted_iota(jnp.int32, (8, WIDTH), 1)
+    sub = lax.broadcasted_iota(jnp.int32, (8, WIDTH), 0)
+    group, inside = lane // BLOCK, lane % BLOCK < TILE
+    own = flipped[...]
+    turned = [pltpu.roll(own, TILE * n, 1) if n else own for n in range(TILE)]
+    forward[...] = jnp.zeros_like(forward)
+    for a in range(TILE):
+        placed = jnp.zeros((8, WIDTH), jnp.float32)
+        for r in range(8):
+            placed = jnp.where((sub == r) & (group == r) & inside, turned[(2 * r - a) % TILE], placed)
+        forward[a : a + 8, :] += placed
+    for t in range(3):
+        x = taps[t]
+        row = sub + 8 * t
+        tap = group - row + TILE
+        placed = jnp.zeros((8, WIDTH), jnp.float32)
+        for n in range(TILE):
+            moved = pltpu.roll(x, TILE * n, 1) if n else x
+            use = ((group + row) % TILE == n) & inside & (tap >= 0) & (tap < TILE)
+            placed = jnp.where(use, moved, placed)
+        adjoint[8 * t : 8 * t + 8, :] = placed
+
+
+def kernel(
+    count, scales, side,
+    image, gradient, weight, psf, facet, slot_of, thresholds, spline,
+    out,
+    xi, xg, xh, current, near, middle, far, psf_all, taps, flipped, base_f, base_a, fh, fl, ah, al,
+    levels, sums, tiles, wide,
+    psf_send, psf_recv, sum_send, sum_recv, tap_send, tap_recv, near_send, near_recv, far_send, far_recv,
+):
+    me = lax.axis_index("rows") * scales + lax.axis_index("scales")
+    barrier = pltpu.get_barrier_semaphore()
+
+    def device(index):
+        return (index // scales, index % scales)
+
+    def peer(k):
+        return (me + k) % count
+
+    def exists(o):
+        return (me + o >= 0) & (me + o < count)
+
+    def greet(k, carry):
+        pl.semaphore_signal(barrier, inc=1, device_id=device(peer(k)), device_id_type=MESH)
+        return carry
+
+    lax.fori_loop(1, count, greet, 0)
+
+    def copy(src, dst, send_sem, recv_sem, index):
+        return pltpu.make_async_remote_copy(
+            src_ref=src, dst_ref=dst, send_sem=send_sem, recv_sem=recv_sem,
+            device_id=device(index), device_id_type=MESH,
+        )
+
+    def share(src, pool, send, recv):
+        def start(k, carry):
+            copy(src, pool.at[me], send.at[k], recv.at[me], peer(k)).start()
+            return carry
+
+        lax.fori_loop(1, count, start, 0)
+
+    def collect(src, pool, send, recv):
+        def wait(k, carry):
+            copy(src, pool.at[peer(k)], send.at[k], recv.at[peer(k)], peer(k)).wait()
+            return carry
+
+        lax.fori_loop(1, count, wait, 0)
+
+    def spread(src, place, send, recv, offsets):
+        for o in offsets:
+
+            @pl.when(exists(o))
+            def _():
+                copy(src, place(-o), send(o), recv(-o), me + o).start()
+
+    def arrive(src, place, send, recv, offsets):
+        for o in offsets:
+
+            @pl.when(exists(o))
+            def _():
+                copy(src, place(o), send(o), recv(o), me + o).wait()
+
+    def near_spread(e, src):
+        args = (src, lambda o: near.at[e, (o + 1) // 2], lambda o: near_send.at[e, (o + 1) // 2],
+                lambda o: near_recv.at[e, (o + 1) // 2], (-1, 1))
+        spread(*args)
+        return lambda: arrive(*args)
+
+    offsets = [sign * o for o in range(1, side + 1) for sign in (-1, 1)]
+
+    def far_spread(e):
+        args = (middle, lambda o: far.at[o + side], lambda o: far_send.at[e, o + side],
+                lambda o: far_recv.at[e, o + side], offsets)
+        spread(*args)
+        return lambda: arrive(*args)
+
+    to_blocks(gradient, xg, tiles)
+    for o in (-1, 1):
+
+        @pl.when(jnp.logical_not(exists(o)))
+        def _():
+            for e in range(near.shape[0]):
+                near[e, (o + 1) // 2] = jnp.zeros(near.shape[2:], jnp.float32)
+            taps[o + 1] = jnp.zeros(taps.shape[1:], jnp.float32)
+
+    for o in offsets:
+
+        @pl.when(jnp.logical_not(exists(o)))
+        def _():
+            far[o + side] = jnp.zeros(far.shape[1:], jnp.float32)
+
+    pl.semaphore_wait(barrier, count - 1)
+    share(psf, psf_all, psf_send, psf_recv)
+    near_done = near_spread(0, xg)
     to_blocks(image, xi, tiles)
-    to_blocks(gradient, xg, tiles)
     to_blocks(weight, xh, tiles)
+    psf_all[me] = psf[...]
+    collect(psf, psf_all, psf_send, psf_recv)
+    for r in range(8):
+        both = psf_all[slot_of[facet[r]]]
+        taps[1, r : r + 1, :] = both[0:1]
+        flipped[r : r + 1, :] = both[1:2]
+    tap_args = (taps.at[1], lambda o: taps.at[o + 1], lambda o: tap_send.at[(o + 1) // 2],
+                lambda o: tap_recv.at[(o + 1) // 2], (-1, 1))
+    spread(*tap_args)
+    arrive(*tap_args)
+    build_bases(taps, flipped, base_f, base_a)
     build_weights(base_f, HALF - 1, fh, fl, wide)
-    build_weights(base_a, HALF, ah, al, wide)
-
-
-def forward_kernel(below, own, above, h, fh, fl, out):
-    out[...] = h[...] * blur([below[...], own[...], above[...]], fh, fl)
-
-
-def adjoint_kernel(below, own, above, g, ah, al, out):
-    out[...] = g[...] + blur([below[...], own[...], above[...]], ah, al)
-
-
-def sums_kernel(below, own, above, h, fh, fl, out):
-    d = own[...]
-    b = blur([below[...], d, above[...]], fh, fl)
-    first = jnp.sum(d * d, axis=0, keepdims=True)
-    second = jnp.sum(h[...] * b * b, axis=0, keepdims=True)
-    out[...] = jnp.concatenate([first, second], axis=0)
-
-
-def shrink_kernel(*refs, count, final):
-    stripes, alive_ref, limits_ref, spline = refs[:count], refs[count], refs[count + 1], refs[count + 2]
-    out, levels = refs[count + 3], refs[count + 4]
-    alive = [alive_ref[t] for t in range(count)]
-    column_cascade(stripes, alive, levels, 8)
-    row_cascade(levels, spline)
-    new = keep(stripes[count // 2][...], levels, [limits_ref[k] for k in range(levels.shape[0])])
-    if final:
-        whole, tiles = refs[count + 5], refs[count + 6]
-        whole[...] = new
-        from_blocks(whole, out, tiles)
-    else:
-        out[...] = new
-
-
-def call(kernel, outs, *args, scratch=(), smem=()):
-    specs = [pl.BlockSpec(memory_space=pltpu.SMEM) if n in smem else VMEM for n in range(len(args))]
-    many = isinstance(outs, list)
-    return pl.pallas_call(
-        kernel,
-        out_shape=outs,
-        in_specs=specs,
-        out_specs=[VMEM] * len(outs) if many else VMEM,
-        scratch_shapes=list(scratch),
-        compiler_params=pltpu.CompilerParams(vmem_limit_bytes=56 * 1024 * 1024),
-    )(*args)
-
-
-def bases(taps, wide_taps):
-    rows = taps.shape[0]
-    flipped = jnp.flip(taps, axis=2)
-    forward = jnp.stack([jnp.pad(flipped[r], ((r, rows - r), (0, 0))) for r in range(rows)], axis=1)
-    padded = jnp.pad(wide_taps, ((0, 0), (rows, rows), (0, 0)))
-    adjoint = jnp.stack(
-        [padded[i, 3 * rows - i : 4 * rows - i] for i in range(3 * rows)], axis=0
-    )
-    widen = lambda x: jnp.pad(x, ((0, 0), (0, 0), (0, BLOCK - TILE))).reshape(3 * rows, WIDTH)
-    return widen(forward), widen(adjoint)
+    alive = [None if t == side else jnp.where(exists(t - side), 1.0, 0.0) for t in range(2 * side + 1)]
+
+    for sweep in range(SUBITERS):
+        if sweep == 0:
+            descent = xg
+        else:
+            descent = middle
+            e = 3 * sweep - 2
+            done = near_spread(e, current_change)
+            done()
+            change = current_change[...]
+            pushed = xh[...] * blur([near[e, 0], change, near[e, 1]], fh, fl)
+            far[side] = pushed
+            near_done = near_spread(e + 1, far.at[side])
+            near_done()
+            middle[...] = xg[...] + blur([near[e + 1, 0], pushed, near[e + 1, 1]], ah, al)
+            near_done = near_spread(e + 2, middle)
+        near_done()
+        e = 3 * sweep
+        d = descent[...]
+        b = blur([near[e, 0], d, near[e, 1]], fh, fl)
+
+        def lanes(x):
+            column = jnp.sum(x, axis=0, keepdims=True)
+            return column[:, :LANES] + column[:, LANES:]
+
+        sums[sweep, me] = jnp.concatenate([lanes(d * d), lanes(xh[...] * b * b)], axis=0)
+        own = sums.at[sweep, me]
+        share(own, sums.at[sweep], sum_send.at[sweep], sum_recv.at[sweep])
+        if sweep == 0:
+            build_weights(base_a, HALF, ah, al, wide)
+        collect(own, sums.at[sweep], sum_send.at[sweep], sum_recv.at[sweep])
+        totals = jnp.sum(jnp.sum(sums[sweep], axis=0), axis=1, keepdims=True)
+        step = totals[0:1] / totals[1:2]
+        start = xi if sweep == 0 else current
+        middle[...] = start[...] - step * d
+        far_done = far_spread(sweep)
+        far_done()
+        stripes = [middle if t == side else far.at[t] for t in range(2 * side + 1)]
+        column_cascade(stripes, alive, levels, 8)
+        row_cascade(levels, spline)
+        new = keep(middle[...], levels, [step * thresholds[k] for k in range(levels.shape[0])])
+        current[...] = new
+        if sweep < SUBITERS - 1:
+            current_change = far.at[side]
+            current_change[...] = new - xi[...]
+    from_blocks(current, out, tiles)
+
+
+MESH = pl.DeviceIdType.MESH
 
 
 def body(image_now, gradient, hessian_weight, psf_tiles, facet_of_row, tile_slot, thresholds):
     band, columns = image_now.shape
     levels = thresholds.shape[0]
     blocks = columns // BLOCK
-    count = lax.axis_size("rows") * lax.axis_size("scales")
-    me = lax.axis_index("rows") * lax.axis_size("scales") + lax.axis_index("scales")
-
-    def from_offset(x, offset):
-        pairs = [(i, i - offset) for i in range(count) if 0 <= i - offset < count]
-        return lax.ppermute(x, AXES, pairs)
-
-    facet_ids = jnp.arange(tile_slot.shape[0], dtype=jnp.int32)
-    slot_rows = jnp.sum(
-        jnp.where(facet_of_row[:, None] == facet_ids[None, :], tile_slot[None, :], 0), axis=1
-    )
-    tiles_in = lax.all_gather(psf_tiles, AXES, axis=0, tiled=True)
-    length = tiles_in.shape[0]
-    onehot = (slot_rows[:, None] == jnp.arange(length, dtype=jnp.int32)[None, :]).astype(jnp.float32)
-    flat = jnp.dot(
-        onehot, tiles_in, precision=lax.Precision.HIGHEST, preferred_element_type=jnp.float32
-    )
-    wide_flat = jnp.concatenate([from_offset(flat, -1), flat, from_offset(flat, 1)], axis=0)
-    base_f, base_a = bases(
-        flat.reshape(band, TILE, TILE), wide_flat.reshape(3 * band, TILE, TILE)
-    )
-    plane = jax.ShapeDtypeStruct((blocks, WIDTH), jnp.float32)
-    table = jax.ShapeDtypeStruct((9, WIDTH, WIDTH), jnp.bfloat16)
-    tiles = pltpu.VMEM((columns // LANES * 8, LANES), jnp.float32)
-    xi, xg, xh, fh, fl, ah, al = call(
-        prepare_kernel,
-        [plane] * 3 + [table] * 4,
-        image_now, gradient, hessian_weight, base_f, base_a,
-        scratch=[tiles, pltpu.VMEM((3, 2, WIDTH, LANES), jnp.float32)],
-    )
-    spline = spline_matrices(levels)
+    scales = lax.axis_size("scales")
+    count = lax.axis_size("rows") * scales
     reach = 2 ** (levels + 1) - 2
     side = -(-reach // band)
-    offsets = list(range(-side, side + 1))
-    alive = jnp.stack([((me + o >= 0) & (me + o < count)).astype(jnp.float32) for o in offsets])
-
-    def around(x):
-        return from_offset(x, -1), x, from_offset(x, 1)
-
-    current = xi
-    for sweep in range(SUBITERS):
-        if sweep == 0:
-            descent = xg
-        else:
-            pushed = call(forward_kernel, plane, *around(current - xi), xh, fh, fl)
-            descent = call(adjoint_kernel, plane, *around(pushed), xg, ah, al)
-        sums = call(
-            sums_kernel, jax.ShapeDtypeStruct((2, WIDTH), jnp.float32), *around(descent), xh, fh, fl
-        )
-        totals = lax.psum(jnp.sum(sums, axis=1), AXES)
-        step_size = totals[0] / totals[1]
-        trial = current - step_size * descent
-        stripes = [from_offset(trial, o) if o else trial for o in offsets]
-        final = sweep == SUBITERS - 1
-        scratch = [pltpu.VMEM((levels, blocks, WIDTH), jnp.float32)]
-        if final:
-            scratch += [pltpu.VMEM((blocks, WIDTH), jnp.float32), tiles]
-        n = len(stripes)
-        current = call(
-            functools.partial(shrink_kernel, count=n, final=final),
-            jax.ShapeDtypeStruct((band, columns), jnp.float32) if final else plane,
-            *stripes, alive, step_size * thresholds, spline,
-            scratch=scratch, smem=(n, n + 1),
-        )
-    return current
+    own = psf_tiles.reshape(TILE, TILE)
+    psf = jnp.stack([own, jnp.flip(own, axis=1)]).reshape(2, TILE * TILE)
+    plane = (blocks, WIDTH)
+    table = pltpu.VMEM((9, WIDTH, WIDTH), jnp.bfloat16)
+    f32 = lambda *shape: pltpu.VMEM(shape, jnp.float32)
+    sem = lambda *shape: pltpu.SemaphoreType.DMA(shape)
+    smem = pl.BlockSpec(memory_space=pltpu.SMEM)
+    exchanges = 3 * SUBITERS - 2
+    return pl.pallas_call(
+        functools.partial(kernel, count, scales, side),
+        out_shape=jax.ShapeDtypeStruct((band, columns), jnp.float32),
+        in_specs=[VMEM] * 4 + [smem] * 3 + [VMEM],
+        out_specs=VMEM,
+        scratch_shapes=[
+            f32(*plane), f32(*plane), f32(*plane), f32(*plane),
+            f32(exchanges, 2, *plane), f32(*plane), f32(2 * side + 1, *plane),
+            f32(count, 2, TILE * TILE), f32(3, 8, TILE * TILE), f32(8, TILE * TILE),
+            f32(3 * band, WIDTH), f32(3 * band, WIDTH), table, table, table, table,
+            f32(levels, *plane), f32(SUBITERS, count, 2, LANES),
+            f32(columns // LANES * 8, LANES), f32(3, 2, WIDTH, LANES),
+            sem(count), sem(count), sem(SUBITERS, count), sem(SUBITERS, count), sem(2), sem(2),
+            sem(exchanges, 2), sem(exchanges, 2),
+            sem(SUBITERS, 2 * side + 1), sem(SUBITERS, 2 * side + 1),
+        ],
+        compiler_params=pltpu.CompilerParams(
+            collective_id=0, has_side_effects=True, vmem_limit_bytes=56 * 1024 * 1024
+        ),
+    )(image_now, gradient, hessian_weight, psf, facet_of_row, tile_slot, thresholds, spline_matrices(levels))
 
 
 def solution(mesh):

time: 315 us -> 144 us (0.46); the launches traced: 311 us -> 144 us
  blocking collectives: 128 us -> 0 us
  Pallas kernels: 51.3 us -> 139 us
  starting transfers between devices: 86.3 us -> 0 us
  waiting for transfers between devices: 28.7 us -> 0 us
  local copies, waits for them, and re-layouts: 8.73 us -> 2.42 us
  between operations: 3.3 us -> 0.01 us
    pallas_call x7 -> x1, Pallas kernels: 51.3 us -> 139 us  [body(): pl.pallas_call(functools.partial(kernel, count, scales, side), out_shape=...]
    ppermute x26 -> x0, starting transfers between devices: 86.3 us -> none  [from_offset(): return lax.ppermute(x, AXES, pairs)]
    psum x2 -> x0, blocking collectives: 84.4 us -> none  [body(): totals = lax.psum(jnp.sum(sums, axis=1), AXES)]
    all_gather x1 -> x0, blocking collectives: 43.4 us -> none  [body(): tiles_in = lax.all_gather(psf_tiles, AXES, axis=0, tiled=True)]
    ppermute x26 -> x0, waiting for transfers between devices: 28.7 us -> none  [from_offset(): return lax.ppermute(x, AXES, pairs)]
  transfers between devices with their start and end apart: 26 -> 0, of which waited for: 14 -> 0; matrix products, arithmetic and copies ran while one was open for 1% -> 0% of each run, Pallas kernels for 0% -> 0%
where the time goes in v2:
time: 144 us
  Pallas kernels  139 us (97%)
  other arithmetic  2.61 us (2%)
  local copies, waits for them, and re-layouts  2.42 us (2%)
    pallas_call x1, Pallas kernels, body(): pl.pallas_call(functools.partial(kernel, count, scales, side), out_shape=...  139 us

profile of v2, /device:TPU:1, one launch (start us, length us, event | category | flops | bytes accessed | tf_op | source)
XLA Modules:
  0.0 144.1 jit_solution(10404928143014159041)
XLA Ops:
  0.0 0.5 broadcast.3
  0.5 1.3 reduce.3
  1.9 0.1 reshape.8
  1.9 0.1 rev.4
  2.0 0.1 stack.6
  2.1 1.3 pad_maximum_fusion.psf
  3.4 139.1 %shard_map.82 = f32[8,8192]{1,0:T(8,128)} custom-call(f32[8,8192]{1,0:T(8,128)} %image.1, f32[8,8192]{1,0:T(8,128)} %gradient.1, f32[8,8192]{1,0:T(8,128)} %weight.1, f32[2,256]{1,0:T(2,128)} %pad_maximum_fusion.psf, s32[8]{0:T(128)} %facet.1, s32[32]{0:T(128)} %slot_of.1, f32[4]{0:T(128)} %thresholds.1, bf16[12,256,256]{2,1,0:T(8,128)(2,1)} %constant.2.clone.spline), custom_call_target="tpu_custom_call" | custom-call | tf_op jit(solution)/shard_map/pallas_call | solution.py:401
  142.5 1.7 %copy.10 = f32[8,8192]{1,0:T(8,128)} copy(f32[8,8192]{1,0:T(8,128)} %shard_map.82) | data formatting | bytes 524288

commit v3 on v2

--- a/solution.py
+++ b/solution.py
@@ -22,12 +22,13 @@
 def spline_matrices(levels):
     w = np.arange(WIDTH)
     same = (w[:, None] // BLOCK) == (w[None, :] // BLOCK)
-    offset = (w[:, None] % BLOCK) - (w[None, :] % BLOCK)
+    place = w % BLOCK
+    nearer = place + np.where(place < BLOCK // 2, BLOCK, -BLOCK)
     planes = []
     for level in range(levels):
         d = 2**level
-        for s in (-1, 0, 1):
-            o = np.abs(offset + BLOCK * s)
+        for column in (place, nearer):
+            o = np.abs(column[:, None] - place[None, :])
             coef = np.where(o == 0, 0.375, np.where(o == d, 0.25, np.where(o == 2 * d, 0.0625, 0.0)))
             planes.append(np.where(same, coef, 0.0))
     return jnp.asarray(np.stack(planes), jnp.bfloat16)
@@ -56,17 +57,19 @@
     return jnp.concatenate([first] + parts[:-1], axis=0)
 
 
+def beside(x):
+    lane = lax.broadcasted_iota(jnp.int32, x.shape, 1) % BLOCK
+    return jnp.where(lane < BLOCK // 2, block_shift(x, 1), block_shift(x, -1))
+
+
 def blur(stripes, high_ref, low_ref):
-    parts = [halves(x) for x in stripes]
     total = None
-    for s in (-1, 0, 1):
-        here = None
-        for t, (high, low) in enumerate(parts):
-            w = high_ref[t * 3 + s + 1]
-            part = dot(high, w) + dot(low, w) + dot(high, low_ref[t * 3 + s + 1])
-            here = part if here is None else here + part
-        here = block_shift(here, s)
-        total = here if total is None else total + here
+    for t, x in enumerate(stripes):
+        for n, y in enumerate((x, beside(x))):
+            high, low = halves(y)
+            w = high_ref[t * 2 + n]
+            part = dot(high, w) + dot(low, w) + dot(high, low_ref[t * 2 + n])
+            total = part if total is None else total + part
     return total
 
 
@@ -108,19 +111,19 @@
     for t in range(3):
         base = base_ref[8 * t : 8 * t + 8, :]
         for w in range(BLOCK):
-            for s in (-1, 0, 1):
+            for n, s in enumerate((0, 1 if w < BLOCK // 2 else -1)):
                 moved = pltpu.roll(base, (w - lead + BLOCK * s) % WIDTH, 1)
                 x = lane - (w - lead + BLOCK * s)
                 kept = jnp.where((x >= 0) & (x < TILE), moved, 0.0)
                 for half in range(2):
-                    wide[s + 1, half, pl.ds(w, 8, stride=BLOCK), :] = kept[
+                    wide[n, half, pl.ds(w, 8, stride=BLOCK), :] = kept[
                         :, half * LANES : (half + 1) * LANES
                     ]
-        for s in range(3):
+        for n in range(2):
             for half in range(2):
-                high, low = halves(wide[s, half])
-                high_ref[t * 3 + s, :, half * LANES : (half + 1) * LANES] = high
-                low_ref[t * 3 + s, :, half * LANES : (half + 1) * LANES] = low
+                high, low = halves(wide[n, half])
+                high_ref[t * 2 + n, :, half * LANES : (half + 1) * LANES] = high
+                low_ref[t * 2 + n, :, half * LANES : (half + 1) * LANES] = low
 
 
 def moved_rows(vregs, rolls, i, d):
@@ -139,16 +142,18 @@
     return jnp.where(lane >= -BLOCK * d, rolled(i), rolled(i - 1))
 
 
-def column_cascade(stripe_refs, alive, levels_ref, step_rows):
-    reach = len(stripe_refs) // 2
+def column_cascade(images, descents, step, alive, levels_ref, step_rows):
+    reach = images.shape[0] // 2
+    wide_step = jnp.broadcast_to(step, (step_rows, LANES))
     levels = levels_ref.shape[0]
 
     def chunk(n, carry):
         rows = pl.ds(pl.multiple_of(n * step_rows, step_rows), step_rows)
         vregs = {}
-        for t, ref in enumerate(stripe_refs):
+        for t in range(images.shape[0]):
             for half in range(2):
-                vregs[2 * t + half] = ref[rows, half * LANES : (half + 1) * LANES]
+                lanes = slice(half * LANES, (half + 1) * LANES)
+                vregs[2 * t + half] = images[t, rows, lanes] - wide_step * descents[t, rows, lanes]
         own = 2 * reach
         for level in range(levels):
             d = 2**level
@@ -167,7 +172,7 @@
                 levels_ref[level, rows, half * LANES : (half + 1) * LANES] = out[own + half]
         return carry
 
-    lax.fori_loop(0, stripe_refs[0].shape[0] // step_rows, chunk, 0)
+    lax.fori_loop(0, images.shape[1] // step_rows, chunk, 0)
 
 
 def row_cascade(levels_ref, spline_ref):
@@ -175,11 +180,12 @@
     for level in range(levels):
 
         def one(k, carry):
-            high, low = halves(levels_ref[k])
+            x = levels_ref[k]
             total = None
-            for s in (-1, 0, 1):
-                w = spline_ref[level * 3 + s + 1]
-                part = block_shift(dot(high, w) + dot(low, w), s)
+            for n, y in enumerate((x, beside(x))):
+                high, low = halves(y)
+                w = spline_ref[level * 2 + n]
+                part = dot(high, w) + dot(low, w)
                 total = part if total is None else total + part
             levels_ref[k] = total
             return carry
@@ -228,7 +234,7 @@
     count, scales, side,
     image, gradient, weight, psf, facet, slot_of, thresholds, spline,
     out,
-    xi, xg, xh, current, near, middle, far, psf_all, taps, flipped, base_f, base_a, fh, fl, ah, al,
+    xh, current, near, far, psf_all, taps, flipped, base_f, base_a, fh, fl, ah, al,
     levels, sums, tiles, wide,
     psf_send, psf_recv, sum_send, sum_recv, tap_send, tap_recv, near_send, near_recv, far_send, far_recv,
 ):
@@ -284,22 +290,20 @@
             def _():
                 copy(src, place(o), send(o), recv(o), me + o).wait()
 
-    def near_spread(e, src):
-        args = (src, lambda o: near.at[e, (o + 1) // 2], lambda o: near_send.at[e, (o + 1) // 2],
-                lambda o: near_recv.at[e, (o + 1) // 2], (-1, 1))
-        spread(*args)
-        return lambda: arrive(*args)
-
-    offsets = [sign * o for o in range(1, side + 1) for sign in (-1, 1)]
-
-    def far_spread(e):
-        args = (middle, lambda o: far.at[o + side], lambda o: far_send.at[e, o + side],
+    def pushed_args(e, src):
+        return (src, lambda o: near.at[e, (o + 1) // 2], lambda o: near_send.at[e, (o + 1) // 2],
+                lambda o: near_recv.at[e, (o + 1) // 2], close)
+
+    close = [-1, 1]
+    distant = [sign * o for o in range(2, side + 1) for sign in (-1, 1)]
+
+    def plane_args(e, offsets):
+        return (far.at[e, side], lambda o: far.at[e, o + side], lambda o: far_send.at[e, o + side],
                 lambda o: far_recv.at[e, o + side], offsets)
-        spread(*args)
-        return lambda: arrive(*args)
-
-    to_blocks(gradient, xg, tiles)
-    for o in (-1, 1):
+
+    to_blocks(gradient, far.at[1, side], tiles)
+    to_blocks(image, far.at[0, side], tiles)
+    for o in close:
 
         @pl.when(jnp.logical_not(exists(o)))
         def _():
@@ -307,16 +311,19 @@
                 near[e, (o + 1) // 2] = jnp.zeros(near.shape[2:], jnp.float32)
             taps[o + 1] = jnp.zeros(taps.shape[1:], jnp.float32)
 
-    for o in offsets:
+    for o in close + distant:
 
         @pl.when(jnp.logical_not(exists(o)))
         def _():
-            far[o + side] = jnp.zeros(far.shape[1:], jnp.float32)
+            for e in range(far.shape[0]):
+                far[e, o + side] = jnp.zeros(far.shape[2:], jnp.float32)
 
     pl.semaphore_wait(barrier, count - 1)
     share(psf, psf_all, psf_send, psf_recv)
-    near_done = near_spread(0, xg)
-    to_blocks(image, xi, tiles)
+    spread(*plane_args(1, close))
+    spread(*plane_args(0, close))
+    spread(*plane_args(1, distant))
+    spread(*plane_args(0, distant))
     to_blocks(weight, xh, tiles)
     psf_all[me] = psf[...]
     collect(psf, psf_all, psf_send, psf_recv)
@@ -333,24 +340,23 @@
     alive = [None if t == side else jnp.where(exists(t - side), 1.0, 0.0) for t in range(2 * side + 1)]
 
     for sweep in range(SUBITERS):
-        if sweep == 0:
-            descent = xg
-        else:
-            descent = middle
-            e = 3 * sweep - 2
-            done = near_spread(e, current_change)
-            done()
-            change = current_change[...]
-            pushed = xh[...] * blur([near[e, 0], change, near[e, 1]], fh, fl)
-            far[side] = pushed
-            near_done = near_spread(e + 1, far.at[side])
-            near_done()
-            middle[...] = xg[...] + blur([near[e + 1, 0], pushed, near[e + 1, 1]], ah, al)
-            near_done = near_spread(e + 2, middle)
-        near_done()
-        e = 3 * sweep
-        d = descent[...]
-        b = blur([near[e, 0], d, near[e, 1]], fh, fl)
+        e = 2 * sweep
+        if sweep > 0:
+            images = [far[0, side + o] for o in (-1, 0, 1)]
+            arrive(*plane_args(e, close))
+            changes = [far[e, side + o] - images[o + 1] for o in (-1, 0, 1)]
+            current[...] = xh[...] * blur(changes, fh, fl)
+            args = pushed_args(sweep - 1, current)
+            spread(*args)
+            spread(*plane_args(e, distant))
+            arrive(*args)
+            pushed = [near[sweep - 1, 0], current[...], near[sweep - 1, 1]]
+            far[e + 1, side] = far[1, side] + blur(pushed, ah, al)
+            spread(*plane_args(e + 1, close))
+            spread(*plane_args(e + 1, distant))
+        arrive(*plane_args(e + 1, close))
+        d = far[e + 1, side]
+        b = blur([far[e + 1, side - 1], d, far[e + 1, side + 1]], fh, fl)
 
         def lanes(x):
             column = jnp.sum(x, axis=0, keepdims=True)
@@ -364,18 +370,19 @@
         collect(own, sums.at[sweep], sum_send.at[sweep], sum_recv.at[sweep])
         totals = jnp.sum(jnp.sum(sums[sweep], axis=0), axis=1, keepdims=True)
         step = totals[0:1] / totals[1:2]
-        start = xi if sweep == 0 else current
-        middle[...] = start[...] - step * d
-        far_done = far_spread(sweep)
-        far_done()
-        stripes = [middle if t == side else far.at[t] for t in range(2 * side + 1)]
-        column_cascade(stripes, alive, levels, 8)
+        if sweep == 0:
+            arrive(*plane_args(e, close))
+        arrive(*plane_args(e, distant))
+        arrive(*plane_args(e + 1, distant))
+        column_cascade(far.at[e], far.at[e + 1], step, alive, levels, 8)
         row_cascade(levels, spline)
-        new = keep(middle[...], levels, [step * thresholds[k] for k in range(levels.shape[0])])
-        current[...] = new
+        trial = far[e, side] - step * far[e + 1, side]
+        new = keep(trial, levels, [step * thresholds[k] for k in range(levels.shape[0])])
         if sweep < SUBITERS - 1:
-            current_change = far.at[side]
-            current_change[...] = new - xi[...]
+            far[e + 2, side] = new
+            spread(*plane_args(e + 2, close))
+        else:
+            current[...] = new
     from_blocks(current, out, tiles)
 
 
@@ -393,26 +400,26 @@
     own = psf_tiles.reshape(TILE, TILE)
     psf = jnp.stack([own, jnp.flip(own, axis=1)]).reshape(2, TILE * TILE)
     plane = (blocks, WIDTH)
-    table = pltpu.VMEM((9, WIDTH, WIDTH), jnp.bfloat16)
+    table = pltpu.VMEM((6, WIDTH, WIDTH), jnp.bfloat16)
     f32 = lambda *shape: pltpu.VMEM(shape, jnp.float32)
     sem = lambda *shape: pltpu.SemaphoreType.DMA(shape)
     smem = pl.BlockSpec(memory_space=pltpu.SMEM)
-    exchanges = 3 * SUBITERS - 2
+    pairs = 2 * SUBITERS
     return pl.pallas_call(
         functools.partial(kernel, count, scales, side),
         out_shape=jax.ShapeDtypeStruct((band, columns), jnp.float32),
         in_specs=[VMEM] * 4 + [smem] * 3 + [VMEM],
         out_specs=VMEM,
         scratch_shapes=[
-            f32(*plane), f32(*plane), f32(*plane), f32(*plane),
-            f32(exchanges, 2, *plane), f32(*plane), f32(2 * side + 1, *plane),
+            f32(*plane), f32(*plane),
+            f32(SUBITERS - 1, 2, *plane), f32(pairs, 2 * side + 1, *plane),
             f32(count, 2, TILE * TILE), f32(3, 8, TILE * TILE), f32(8, TILE * TILE),
             f32(3 * band, WIDTH), f32(3 * band, WIDTH), table, table, table, table,
             f32(levels, *plane), f32(SUBITERS, count, 2, LANES),
-            f32(columns // LANES * 8, LANES), f32(3, 2, WIDTH, LANES),
+            f32(columns // LANES * 8, LANES), f32(2, 2, WIDTH, LANES),
             sem(count), sem(count), sem(SUBITERS, count), sem(SUBITERS, count), sem(2), sem(2),
-            sem(exchanges, 2), sem(exchanges, 2),
-            sem(SUBITERS, 2 * side + 1), sem(SUBITERS, 2 * side + 1),
+            sem(SUBITERS - 1, 2), sem(SUBITERS - 1, 2),
+            sem(pairs, 2 * side + 1), sem(pairs, 2 * side + 1),
         ],
         compiler_params=pltpu.CompilerParams(
             collective_id=0, has_side_effects=True, vmem_limit_bytes=56 * 1024 * 1024

time: 144 us -> 168 us (1.17); the launches traced: 144 us -> 165 us
  Pallas kernels: 139 us -> 162 us
    pallas_call x1, Pallas kernels: 139 us -> 162 us  [body(): pl.pallas_call(functools.partial(kernel, count, scales, side), out_shape=...]
where the time goes in v3:
time: 168 us; the launch traced here: 165 us
  Pallas kernels  162 us (96%)
  local copies, waits for them, and re-layouts  2.59 us (2%)
    pallas_call x1, Pallas kernels, body(): pl.pallas_call(functools.partial(kernel, count, scales, side), out_shape=...  162 us

profile of v3, /device:TPU:1, one launch (start us, length us, event | category | flops | bytes accessed | tf_op | source)
XLA Modules:
  0.0 165.4 jit_solution(3873241438634040840)
XLA Ops:
  0.0 0.0 copy-start
  0.0 0.5 broadcast.3
  0.5 0.2 copy-done
  0.7 0.7 reduce.3
  1.3 0.1 reshape.8
  1.4 0.1 rev.4
  1.5 0.1 stack.6
  1.6 0.6 pad_maximum_fusion.psf
  2.2 161.5 %shard_map.82 = f32[8,8192]{1,0:T(8,128)} custom-call(f32[8,8192]{1,0:T(8,128)} %image.1, f32[8,8192]{1,0:T(8,128)} %gradient.1, f32[8,8192]{1,0:T(8,128)} %weight.1, f32[2,256]{1,0:T(2,128)} %pad_maximum_fusion.psf, s32[8]{0:T(128)} %facet.1, s32[32]{0:T(128)} %slot_of.1, f32[4]{0:T(128)} %thresholds.1, bf16[8,256,256]{2,1,0:T(8,128)(2,1)} %constant.2.clone.spline), custom_call_target="tpu_custom_call" | custom-call | tf_op jit(solution)/shard_map/pallas_call | solution.py:408
  163.7 1.7 %copy.10 = f32[8,8192]{1,0:T(8,128)} copy(f32[8,8192]{1,0:T(8,128)} %shard_map.82) | data formatting | bytes 524288
Async XLA Ops:
  0.0 0.7 copy-start
